TPU v7x, 256 devices: a whole 4x4x8 slice. The times are simulated.
256 devices in a mesh: section: 2 (over x_lo), dec: 32 (over x_hi, z, core), row: 4 (over y).
Axes of the slice: x: 4 (x_hi: 2, x_lo: 2; x = x_hi * 2 + x_lo), y: 4, z: 8, core: 2. Of those that a mesh axis runs over, the one named last changes fastest.
Arguments:
- hidden: bfloat16 [64, 4, 16, 8, 5120], P('dec', None, 'row', None, 'section'), may hold values from -12 to 12
- head_weight: bfloat16 [5120, 64], P('section'), may hold values from -0.078125 to 0.078125
- head_bias: float32 [64], replicated, may hold values from -3 to 3
- lat_cache: bfloat16 [64, 2, 32, 16, 16], P('dec', None, 'row'), may hold values from -6 to 6
- mid_cache: bfloat16 [64, 2, 32, 16, 512], P('dec', None, 'row', None, 'section'), may hold values from -6 to 6
- moves: int32 [64], replicated, may hold values from 0 to 63, each once
- span_index: int32 [64], P('dec'), may hold values from 0 to 3
- conv_in_weight: bfloat16 [3, 3, 3, 16, 512], P(None, None, None, None, 'section'), may hold values from -0.3125 to 0.3125
- conv_in_bias: float32 [512], P('section'), may hold values from -3 to 3
- gn_gain: float32 [512], P('section'), may hold values from 0.25 to 1.75
- gn_bias: float32 [512], P('section'), may hold values from -3 to 3
- mid_weight: bfloat16 [3, 3, 3, 512, 512], P(None, None, None, None, 'section'), may hold values from -0.0546875 to 0.0546875
- mid_bias: float32 [512], P('section'), may hold values from -3 to 3
Outputs:
- decoded: bfloat16 [64, 4, 32, 16, 512], P('dec', None, 'row', None, 'section')
- new_lat_cache: bfloat16 [64, 2, 32, 16, 16], P('dec', None, 'row')
- new_mid_cache: bfloat16 [64, 2, 32, 16, 512], P('dec', None, 'row', None, 'section')
Inputs may be any that keep to these rules, and one draw needn't show every extreme that they name: moves holds each of the 64 slots once.
All inputs are finite; a program needn't handle non-finite values.
Results may differ from a plain program's by a relative error of at most 0.012.
Values may be sent and summed in bfloat16 or wider, within the bound.
No kernel may reach another device: no remote copies, remote signals or barrier semaphores. Data moves between devices by JAX's collectives and lax.ppermute only.
A program may use at most 128 MiB of HBM per device.

v0:
```python
import functools

import jax
import jax.numpy as jnp
from jax import lax
from jax.experimental import pallas as pl
from jax.experimental.pallas import tpu as pltpu
from jax.sharding import PartitionSpec as P

CZ = 16
C = 512
GROUPS = 32
CACHE = 2
SWAP = [(0, 1), (1, 0)]
VMEM = pl.BlockSpec(memory_space=pltpu.VMEM)
SMEM = pl.BlockSpec(memory_space=pltpu.SMEM)
ANY = pl.BlockSpec(memory_space=pl.ANY)
F32 = jnp.float32
BF16 = jnp.bfloat16


def call(kernel, name, out_shape, in_specs, out_specs=None, scratch=(), aliases=None, limit=48):
    return pl.pallas_call(
        kernel,
        out_shape=out_shape,
        in_specs=in_specs,
        out_specs=VMEM if out_specs is None else out_specs,
        scratch_shapes=scratch,
        input_output_aliases=aliases or {},
        compiler_params=pltpu.CompilerParams(vmem_limit_bytes=limit << 20),
        name=name,
    )


def head_kernel(hidden_ref, weight_ref, out_ref):
    product = jnp.dot(hidden_ref[...], weight_ref[...], preferred_element_type=F32)
    for frame in range(out_ref.shape[0]):
        for q in range(2):
            parts = [
                product[(frame * 4 + i) * 8 : (frame * 4 + i + 1) * 8, q * 32 : (q + 1) * 32]
                for i in range(4)
            ]
            out_ref[frame, pl.ds(q, 8, stride=2), :] = jnp.concatenate(parts, axis=1)


def pack_kernel(lat_ref, mid_ref, out_ref):
    both = []
    for frame in range(2):
        rows = [lat_ref[k, frame, r] for k in range(2) for r in range(8)]
        both.append(jnp.concatenate(rows, axis=1))
    for piece in range(16):
        frame, row = divmod(piece, 8)
        for k in range(2):
            out_ref[piece, k * 16 : (k + 1) * 16, :] = mid_ref[k, frame, row]
        for frame in range(2):
            out_ref[piece, 32 + frame * 16 : 48 + frame * 16, :] = both[frame]


def pick_kernel(
    me_ref, moves_ref, span_ref, got_ref, twin_ref, part_ref, rest_ref, bias_ref, send_ref, x_ref
):
    dec = me_ref[0]
    core = dec % 2
    hosts = got_ref.shape[0]

    def place(slot, write):
        mine = (slot // 2) % 2 == core

        @pl.when(mine)
        def _():
            write(got_ref, slot // 4, slot % 2)

        @pl.when(jnp.logical_not(mine))
        def _():
            write(twin_ref, slot // 4, slot % 2)

    for host in range(hosts):
        for k in range(2):

            def write(ref, source, which, host=host, k=k):
                value = ref[source, pl.ds(pl.multiple_of(which * 16, 16), 16), :]
                for side in range(2):
                    send_ref[side * hosts + host, k * 16 : (k + 1) * 16, :] = value

            place(moves_ref[4 * host + 2 * core + k], write)
    for k in range(2):
        live = (span_ref[k] > 0).astype(F32)

        def write_lat(ref, source, which, k=k, live=live):
            for frame in range(2):
                lat = ref[
                    source,
                    32 + frame * 16 : 48 + frame * 16,
                    pl.ds(pl.multiple_of(which * 128, 128), 128),
                ]
                x_ref[k, frame] = (lat.astype(F32) * live).astype(BF16)

        place(moves_ref[2 * dec + k], write_lat)
        for f in range(4):
            latent = part_ref[k * 4 + f] + rest_ref[k * 4 + f] + bias_ref[...]
            x_ref[k, 2 + f] = latent.astype(BF16)


def shifted(value, step):
    line = lax.broadcasted_iota(jnp.int32, value.shape, 0)
    edge = 0 if step == 1 else value.shape[0] - 1
    moved = pltpu.roll(value, step % value.shape[0], axis=0)
    return jnp.where(line == edge, 0.0, moved)


def first_kernel(x_ref, low_ref, high_ref, weight_ref, bias_ref, first_ref, stats_ref, lat_ref, taps):
    taps[...] = jnp.zeros_like(taps)

    def fill(index, _):
        k, f = index // 6, index % 6
        wide = jnp.concatenate(
            [low_ref[k, f][:, 96:], x_ref[k, f], high_ref[k, f][:, :32]], axis=1
        ).astype(F32)
        for e, value in enumerate((shifted(wide, 1), wide, shifted(wide, -1))):
            value = value.astype(BF16)
            for r in range(10):
                taps[index, r, :, e * 48 : (e + 1) * 48] = value[:, 16 * r : 16 * r + 48]
        return 0

    lax.fori_loop(0, 12, fill, 0)
    for k in range(2):
        total = jnp.zeros((640, C), F32) + bias_ref[...]
        for a in range(3):
            total = total + jnp.dot(
                taps[k * 6 + a : k * 6 + a + 4].reshape(640, 256),
                weight_ref[a],
                preferred_element_type=F32,
            )
        rounded = total.astype(BF16).reshape(4, 10, 16, C)
        first_ref[k] = rounded
        own = rounded[:, 1:9].reshape(512, C).astype(F32)
        stats_ref[k : k + 1, :] = jnp.sum(own, 0, keepdims=True)
        stats_ref[2 + k : 3 + k, :] = jnp.sum(own * own, 0, keepdims=True)
        for f in range(2):
            for r in range(8):
                lat_ref[k, f, r] = x_ref[k, 4 + f][:, 16 * r : 16 * r + 16]


def group_sum(value):
    lane = lax.broadcasted_iota(jnp.int32, value.shape, 1)
    size = value.shape[1]
    for step in (1, 2, 4, 8):
        ahead = pltpu.roll(value, size - step, axis=1)
        behind = pltpu.roll(value, step, axis=1)
        value = value + jnp.where((lane // step) % 2 == 0, ahead, behind)
    return value


def spread_taps(taps, index, row, value):
    width = value.shape[1]
    for e, moved in enumerate((shifted(value, 1), value, shifted(value, -1))):
        taps[index, row, :, e * width : (e + 1) * width] = moved.astype(BF16)


def block_kernel(
    count,
    me_ref,
    first_ref,
    own_ref,
    near_ref,
    far_ref,
    back_ref,
    vectors_ref,
    bias_ref,
    weight_ref,
    decoded_ref,
    early_ref,
    cache_ref,
    taps,
    weight,
    total,
    sems,
):
    section, row = me_ref[1], me_ref[2]
    copies = [
        pltpu.make_async_copy(weight_ref.at[i], weight.at[i], sems.at[i]) for i in range(9)
    ]
    for copy in copies:
        copy.start()
    sums = group_sum(own_ref[...] + near_ref[...] + far_ref[...] + back_ref[...]) / count
    mean = sums[0:2]
    scale = lax.rsqrt(sums[2:4] - mean * mean + 1e-05) * vectors_ref[1:2]
    for k in range(2):
        centre, factor = mean[k : k + 1], scale[k : k + 1]

        def fill(index, _):
            f, r = index // 10, index % 10
            value = (first_ref[k, f, r].astype(F32) - centre) * factor + vectors_ref[2:3]
            value = 0.5 * value * (1.0 + jnp.tanh(0.5 * value))
            line = row * 8 + r - 1
            value = jnp.where((line >= 0) & (line < 32), value, 0.0)
            spread_taps(taps, k * 4 + f, r, value)
            return 0

        lax.fori_loop(0, 40, fill, 0, unroll=2)
    start = pl.multiple_of(section * 256, 256)
    for k in range(2):
        for t in range(4):
            total[k * 4 + t] = (
                first_ref[k, t, 1:9, :, pl.ds(start, 256)].astype(F32).reshape(128, 256)
                + bias_ref[...]
            )
        for f in range(2):
            cache_ref[k, f] = taps[k * 4 + 2 + f, 1:9, :, pl.ds(C + start, 256)]
    for a in range(3):
        frames = 2 + a
        for b in range(3):
            copies[a * 3 + b].wait()
            for k in range(2):
                lhs = taps[k * 4 : k * 4 + frames, b : b + 8].reshape(frames * 128, 3 * C)
                part = jnp.dot(lhs, weight[a * 3 + b], preferred_element_type=F32)
                total[k * 4 + 2 - a : k * 4 + 4] += part.reshape(frames, 128, 256)
    for k in range(2):
        early_ref[k] = total[k * 4 : k * 4 + 2]
        for t in range(2, 4):
            decoded_ref[k, t] = total[k * 4 + t].astype(BF16).reshape(8, 16, 256)


def cache_kernel(
    span_ref,
    pieces_ref,
    low_ref,
    high_ref,
    early_ref,
    weight_ref,
    decoded_ref,
    out_ref,
    taps,
    weight,
    total,
    rounded,
    sems,
    done,
):
    copies = [
        pltpu.make_async_copy(weight_ref.at[i], weight.at[i], sems.at[i]) for i in range(6)
    ]
    for copy in copies:
        copy.start()
    for k in range(2):
        live = (span_ref[k] > 0).astype(F32)
        rows = slice(k * 16, k * 16 + 16)

        def put(frame, r, left, right):
            value = jnp.concatenate([left, right], axis=1).astype(F32) * live
            spread_taps(taps, k * 2 + frame, r, value)

        for frame in range(2):
            put(frame, 0, low_ref[0, frame, rows], low_ref[1, frame, rows])
            put(frame, 9, high_ref[0, frame, rows], high_ref[1, frame, rows])

        def fill(index, _):
            frame, r = index // 8, index % 8
            put(frame, r + 1, pieces_ref[index, rows], pieces_ref[16 + index, rows])
            return 0

        lax.fori_loop(0, 16, fill, 0, unroll=2)
    total[...] = early_ref[...].reshape(total.shape)
    for a in range(2):
        frames = 2 - a
        for b in range(3):
            copies[a * 3 + b].wait()
            for k in range(2):
                lhs = taps[k * 2 + a : k * 2 + 2, b : b + 8].reshape(frames * 128, 3 * C)
                part = jnp.dot(lhs, weight[a * 3 + b], preferred_element_type=F32)
                total[k * 2 : k * 2 + frames] += part.reshape(frames, 128, 256)
    outs = []
    for k in range(2):
        rounded[k] = total[k * 2 : k * 2 + 2].astype(BF16).reshape(2, 8, 16, 256)
        outs.append(pltpu.make_async_copy(rounded.at[k], out_ref.at[k, pl.ds(0, 2)], done.at[k]))
        outs[k].start()
    for copy in outs:
        copy.wait()


def beside(block):
    count = lax.axis_size("row")
    down = [(i, i + 1) for i in range(count - 1)]
    up = [(i + 1, i) for i in range(count - 1)]
    return down, up


def shards(
    hidden,
    head_weight,
    head_bias,
    lat_cache,
    mid_cache,
    moves,
    span_index,
    conv_in_weight,
    conv_in_bias,
    gn_gain,
    gn_bias,
    mid_weight,
    mid_bias,
):
    streams, frames, half_rows, half_cols, width_part = hidden.shape
    rows, cols = 2 * half_rows, 2 * half_cols
    part = conv_in_weight.shape[-1]
    section = lax.axis_index("section")
    dec = lax.axis_index("dec")
    row = lax.axis_index("row")
    bands = lax.axis_size("row")
    hosts = lax.axis_size("dec") // 2
    down, up = beside(None)
    shape = jax.ShapeDtypeStruct
    me = jnp.stack([dec, section, row]).astype(jnp.int32)

    send = call(
        pack_kernel, "pack", shape((hosts, 64, part), BF16), [VMEM, VMEM]
    )(lat_cache, mid_cache)
    spread = [[2 * j + c for j in range(hosts)] for c in range(2)]
    got = lax.all_to_all(send, "dec", 0, 0, axis_index_groups=spread)
    def whole(own):
        other = lax.ppermute(own, "section", SWAP)
        return jnp.where(
            section == 0,
            jnp.concatenate([own, other], -1),
            jnp.concatenate([other, own], -1),
        )

    in_weight = whole(conv_in_weight.transpose(0, 2, 1, 3, 4).reshape(3, 9 * CZ, part))
    in_weight = jnp.pad(in_weight, ((0, 0), (0, 256 - 9 * CZ), (0, 0)))
    vectors = whole(jnp.stack([conv_in_bias, gn_gain, gn_bias]))

    columns = head_weight.reshape(width_part, 2, 2, CZ).transpose(0, 2, 1, 3).reshape(width_part, -1)
    bias = head_bias.reshape(2, 2, CZ).transpose(1, 0, 2).reshape(1, 2, 1, 2 * CZ)
    bias = jnp.broadcast_to(bias, (half_cols, 2, half_rows, 2 * CZ)).reshape(cols, rows * CZ)
    partial = call(
        head_kernel, "head", shape((streams * frames, cols, rows * CZ), F32), [VMEM, VMEM]
    )(hidden.reshape(-1, width_part), columns)
    rest = lax.ppermute(partial, "section", SWAP)

    got, rest, in_weight, vectors = lax.optimization_barrier((got, rest, in_weight, vectors))
    twin = lax.ppermute(got, "dec", [(i, i ^ 1) for i in range(2 * hosts)])
    back, x_in = call(
        pick_kernel,
        "pick",
        (
            shape((2 * hosts, 32, part), BF16),
            shape((streams, CACHE + frames, cols, rows * CZ), BF16),
        ),
        [SMEM, SMEM, SMEM] + [VMEM] * 5,
        (VMEM, VMEM),
    )(me, moves, span_index, got, twin, partial, rest, bias)
    gather = [
        [s * 2 * hosts + 2 * j + c for s in range(2) for j in range(hosts)] for c in range(2)
    ]
    pieces = lax.all_to_all(back, ("section", "dec"), 0, 0, axis_index_groups=gather)

    low = lax.ppermute(x_in, "row", down)
    high = lax.ppermute(x_in, "row", up)
    first, stats, new_lat = call(
        first_kernel,
        "first",
        (
            shape((streams, frames, rows + 2, cols, 2 * part), BF16),
            shape((4, 2 * part), F32),
            shape((streams, CACHE, rows, cols, CZ), BF16),
        ),
        [VMEM] * 5,
        (VMEM, VMEM, VMEM),
        [pltpu.VMEM((streams * (CACHE + frames), rows + 2, cols, 256), BF16)],
    )(x_in, low, high, in_weight, vectors[0:1])
    others = [
        lax.ppermute(stats, "row", [(i, (i + shift) % bands) for i in range(bands)])
        for shift in range(1, bands)
    ]
    pieces, new_lat = lax.optimization_barrier((pieces, new_lat))
    edges = pieces.reshape(2, CACHE, rows, 32, part)
    low_mid = lax.ppermute(edges[:, :, rows - 1], "row", down)
    others, edge = lax.optimization_barrier((others, edges[:, :, 0]))
    high_mid = lax.ppermute(edge, "row", up)
    taps_weight = mid_weight.reshape(9, 3 * 2 * part, part)
    count = float(frames * rows * bands * cols * (C // GROUPS))
    decoded, early, new_mid = call(
        functools.partial(block_kernel, count),
        "block",
        (
            shape((streams, frames, rows, cols, part), BF16),
            shape((streams, CACHE, rows * cols, part), F32),
            shape((streams, CACHE, rows, cols, part), BF16),
        ),
        [SMEM] + [VMEM] * 7 + [ANY],
        (VMEM, VMEM, VMEM),
        [
            pltpu.VMEM((streams * frames, rows + 2, cols, 3 * 2 * part), BF16),
            pltpu.VMEM((9, 3 * 2 * part, part), BF16),
            pltpu.VMEM((streams * frames, rows * cols, part), F32),
            pltpu.SemaphoreType.DMA((9,)),
        ],
    )(me, first, stats, *others, vectors, mid_bias.reshape(1, part), taps_weight)

    decoded = call(
        cache_kernel,
        "cache",
        shape(decoded.shape, BF16),
        [SMEM] + [VMEM] * 4 + [ANY, ANY],
        ANY,
        [
            pltpu.VMEM((streams * CACHE, rows + 2, cols, 3 * 2 * part), BF16),
            pltpu.VMEM((6, 3 * 2 * part, part), BF16),
            pltpu.VMEM((streams * CACHE, rows * cols, part), F32),
            pltpu.VMEM((streams, CACHE, rows, cols, part), BF16),
            pltpu.SemaphoreType.DMA((6,)),
            pltpu.SemaphoreType.DMA((2,)),
        ],
        {6: 0},
    )(span_index, pieces, low_mid, high_mid, early, taps_weight, decoded)
    return (decoded, new_lat, new_mid)


def solution(mesh):
    placed = (
        P("dec", None, "row", None, "section"),
        P("section", None),
        P(),
        P("dec", None, "row", None, None),
        P("dec", None, "row", None, "section"),
        P(),
        P("dec"),
        P(None, None, None, None, "section"),
        P("section"),
        P("section"),
        P("section"),
        P(None, None, None, None, "section"),
        P("section"),
    )
    return jax.shard_map(
        shards,
        mesh=mesh,
        in_specs=placed,
        out_specs=(
            P("dec", None, "row", None, "section"),
            P("dec", None, "row", None, None),
            P("dec", None, "row", None, "section"),
        ),
        check_vma=False,
    )
```

profile of v0, /device:TPU:2, one launch (start us, length us, event | category | flops | bytes accessed | tf_op | source)
XLA Modules:
  0.0 84.8 jit_solution(9215289267963898007)
XLA Ops:
  0.6 0.0 copy-start.1
  0.6 0.9 %copy-done.1 = bf16[2,2,8,16,256]{4,3,2,1,0:T(8,128)(2,1)S(1)} copy-done((bf16[2,2,8,16,256]{4,3,2,1,0:T(8,128)(2,1)S(1)}, bf16[2,2,8,16,256]{4,3,2,1,0:T(8,128)(2,1)}, u32[]{:S(2)}) %copy-start.1) | copy-done | bytes 262168
  1.6 0.0 copy-start.2
  1.6 0.9 %copy-done.2 = bf16[2,2,8,16,16]{4,3,2,1,0:T(8,128)(2,1)S(1)} copy-done((bf16[2,2,8,16,16]{4,3,2,1,0:T(8,128)(2,1)S(1)}, bf16[2,2,8,16,16]{4,3,2,1,0:T(8,128)(2,1)}, u32[]{:S(2)}) %copy-start.2) | copy-done | bytes 16408
  2.5 0.0 copy-start.7
  2.5 0.0 copy-start.8
  2.5 0.0 copy-start.9
  2.5 0.0 copy-start.10
  2.5 0.0 copy-start.6
  2.5 0.9 %pack.1 = bf16[16,64,256]{2,1,0:T(8,128)(2,1)} custom-call(bf16[2,2,8,16,16]{4,3,2,1,0:T(8,128)(2,1)S(1)} %copy-done.2, bf16[2,2,8,16,256]{4,3,2,1,0:T(8,128)(2,1)S(1)} %copy-done.1), custom_call_target="tpu_custom_call" | custom-call | tf_op jit(solution)/shard_map/pack/pallas_call | solution.py:315
  3.4 10.1 %all-to-all-start = ((bf16[16,64,256]{2,1,0:T(8,128)(2,1)}), bf16[16,64,256]{2,1,0:T(8,128)(2,1)S(1)}, u32[]{:S(2)}, u32[]{:S(2)}) async-start(bf16[16,64,256]{2,1,0:T(8,128)(2,1)} %pack.1), calls=%async_computation | async-start | bytes 1048576 | tf_op jit(solution)/shard_map/all_to_all | solution.py:319
  13.6 0.0 copy-start
  13.6 0.0 copy-done.7
  13.6 1.5 %collective-permute-start.1 = (bf16[3,144,256]{2,1,0:T(8,128)(2,1)S(1)}, bf16[3,144,256]{2,1,0:T(8,128)(2,1)S(1)}, u32[]{:S(2)}, u32[]{:S(2)}) collective-permute-start(bf16[3,144,256]{2,1,0:T(8,128)(2,1)S(1)} %bitcast.31), channel_id=1, source_target_pairs={{0,128},{128,0},{1,129},{129,1},{2,130},{130,2},{3,131},{131,3},{4... | collective-permute-start | bytes 663560 | tf_op jit(solution)/shard_map/ppermute | solution.py:321
  15.1 0.0 copy-done.8
  15.1 0.0 copy-done.9
  15.1 0.0 copy-done.10
  15.1 0.7 collective-permute-start.2
  15.8 0.0 copy-done.6
  15.8 0.3 copy.26.weight_ref
  16.2 0.0 copy-done
  16.2 0.6 head.1.part_ref
  16.7 0.0 copy-start.11
  16.8 0.0 copy-start.3
  16.8 0.0 copy-start.5
  16.8 1.5 %collective-permute-start = (f32[8,16,128]{2,1,0:T(8,128)S(1)}, f32[8,16,128]{2,1,0:T(8,128)S(1)}, u32[]{:S(2)}, u32[]{:S(2)}) collective-permute-start(f32[8,16,128]{2,1,0:T(8,128)S(1)} %head.1.part_ref), channel_id=1, source_target_pairs={{0,128},{128,0},{1,129},{129,1},{2,130},{130,2},{3,131},{131,3},{4... | collective-permute-start | bytes 196616 | tf_op jit(solution)/shard_map/ppermute | solution.py:338
  18.3 6.8 %collective-permute-done.2 = f32[3,256]{1,0:T(4,128)S(1)} collective-permute-done((f32[3,256]{1,0:T(4,128)S(1)}, f32[3,256]{1,0:T(4,128)S(1)}, u32[]{:S(2)}, u32[]{:S(2)}) %collective-permute-start.2) | collective-permute-done | bytes 3104 | tf_op jit(solution)/shard_map/ppermute | solution.py:321
  25.1 0.0 collective-permute-done.1
  25.1 0.1 maximum_select_fusion
  25.2 0.1 pad.4.weight_ref
  25.3 1.5 %collective-permute-done.rest_ref = f32[8,16,128]{2,1,0:T(8,128)S(1)} collective-permute-done((f32[8,16,128]{2,1,0:T(8,128)S(1)}, f32[8,16,128]{2,1,0:T(8,128)S(1)}, u32[]{:S(2)}, u32[]{:S(2)}) %collective-permute-start) | collective-permute-done | bytes 65568 | tf_op jit(solution)/shard_map/ppermute | solution.py:338
  26.8 4.0 %all-to-all-done.got_ref = bf16[16,64,256]{2,1,0:T(8,128)(2,1)S(1)} async-done(((bf16[16,64,256]{2,1,0:T(8,128)(2,1)}), bf16[16,64,256]{2,1,0:T(8,128)(2,1)S(1)}, u32[]{:S(2)}, u32[]{:S(2)}) %all-to-all-start) | async-done | bytes 524320 | tf_op jit(solution)/shard_map/all_to_all | solution.py:319
  30.8 0.0 collective-permute-start.3
  30.8 0.0 copy-done.11
  30.8 0.1 reshape.39
  30.8 0.1 broadcast_in_dim.7
  30.9 0.1 reshape.40.bias_ref
  31.0 0.1 pad_add_fusion.me_ref
  31.1 1.6 %collective-permute-done.3.twin_ref = bf16[16,64,256]{2,1,0:T(8,128)(2,1)S(1)} collective-permute-done((bf16[16,64,256]{2,1,0:T(8,128)(2,1)S(1)}, bf16[16,64,256]{2,1,0:T(8,128)(2,1)S(1)}, u32[]{:S(2)}, u32[]{:S(2)}) %collective-permute-start.3) | collective-permute-done | bytes 524320 | tf_op jit(solution)/shard_map/ppermute | solution.py:341
  32.7 0.0 copy-done.3
  32.7 0.0 copy-done.5
  32.7 2.4 %pick.1 = (bf16[32,32,256]{2,1,0:T(8,128)(2,1)}, bf16[2,6,16,128]{3,2,1,0:T(8,128)(2,1)S(1)}) custom-call(s32[3]{0:T(128)S(1)} %pad_add_fusion.me_ref, s32[64]{0:T(128)S(1)} %copy-done.5, s32[2]{0:T(128)S(1)} %copy-done.3, bf16[16,64,256]{2,1,0:T(8,128)(2,1)S(1)} %all-to-all-done.got_ref, bf16[16,64,256]{2,1,0:T(8,128)(2,1)S(1)} %collective-permute-done.3.twin_ref, ...), custom_call_target="tpu_custom_call" | custom-call | tf_op jit(solution)/shard_map/pick/pallas_call | solution.py:342
  35.0 0.0 copy-start.4
  35.0 7.4 %all-to-all-start.1 = ((bf16[32,32,256]{2,1,0:T(8,128)(2,1)}), bf16[32,32,256]{2,1,0:T(8,128)(2,1)S(1)}, u32[]{:S(2)}, u32[]{:S(2)}) async-start(bf16[32,32,256]{2,1,0:T(8,128)(2,1)} %get-tuple-element.23), calls=%async_computation.1 | async-start | bytes 1048576 | tf_op jit(solution)/shard_map/all_to_all | solution.py:355
  42.5 1.3 %collective-permute-start.5 = (bf16[2,6,16,128]{3,2,1,0:T(8,128)(2,1)S(1)}, bf16[2,6,16,128]{3,2,1,0:T(8,128)(2,1)S(1)}, u32[]{:S(2)}, u32[]{:S(2)}) collective-permute-start(bf16[2,6,16,128]{3,2,1,0:T(8,128)(2,1)S(1)} %get-tuple-element.24.x_ref), channel_id=1, source_target_pairs={{1,0},{2,1},{3,2},{5,4},{6,5},{7,6},{9,8},{10,9},{11,10},{13,12},{... | collective-permute-start | bytes 147464 | tf_op jit(solution)/shard_map/ppermute | solution.py:358
  43.8 4.5 %collective-permute-start.4 = (bf16[2,6,16,128]{3,2,1,0:T(8,128)(2,1)S(1)}, bf16[2,6,16,128]{3,2,1,0:T(8,128)(2,1)S(1)}, u32[]{:S(2)}, u32[]{:S(2)}) collective-permute-start(bf16[2,6,16,128]{3,2,1,0:T(8,128)(2,1)S(1)} %get-tuple-element.24.x_ref), channel_id=1, source_target_pairs={{0,1},{1,2},{2,3},{4,5},{5,6},{6,7},{8,9},{9,10},{10,11},{12,13},{... | collective-permute-start | bytes 147464 | tf_op jit(solution)/shard_map/ppermute | solution.py:357
  48.3 0.1 collective-permute-done.5.high_ref
  48.4 1.6 %collective-permute-done.4.low_ref = bf16[2,6,16,128]{3,2,1,0:T(8,128)(2,1)S(1)} collective-permute-done((bf16[2,6,16,128]{3,2,1,0:T(8,128)(2,1)S(1)}, bf16[2,6,16,128]{3,2,1,0:T(8,128)(2,1)S(1)}, u32[]{:S(2)}, u32[]{:S(2)}) %collective-permute-start.4) | collective-permute-done | bytes 49184 | tf_op jit(solution)/shard_map/ppermute | solution.py:357
  50.1 4.3 %first.1 = (bf16[2,4,10,16,512]{4,3,2,1,0:T(8,128)(2,1)S(1)}, f32[4,512]{1,0:T(4,128)S(1)}, bf16[2,2,8,16,16]{4,3,2,1,0:T(8,128)(2,1)}) custom-call(bf16[2,6,16,128]{3,2,1,0:T(8,128)(2,1)S(1)} %get-tuple-element.24.x_ref, bf16[2,6,16,128]{3,2,1,0:T(8,128)(2,1)S(1)} %collective-permute-done.4.low_ref, ...), custom_call_target="tpu_custom_call" | custom-call | tf_op jit(solution)/shard_map/first/pallas_call | solution.py:359
  54.4 4.1 %collective-permute-start.9 = (f32[4,512]{1,0:T(4,128)S(1)}, f32[4,512]{1,0:T(4,128)S(1)}, u32[]{:S(2)}, u32[]{:S(2)}) collective-permute-start(f32[4,512]{1,0:T(4,128)S(1)} %get-tuple-element.29.own_ref), channel_id=1, source_target_pairs={{0,3},{1,0},{2,1},{3,2},{4,7},{5,4},{6,5},{7,6},{8,11},{9,8},{10,9... | collective-permute-start | bytes 24584 | tf_op jit(solution)/shard_map/ppermute | solution.py:372
  58.5 0.3 collective-permute-start.8
  58.8 1.0 %collective-permute-start.7 = (f32[4,512]{1,0:T(4,128)S(1)}, f32[4,512]{1,0:T(4,128)S(1)}, u32[]{:S(2)}, u32[]{:S(2)}) collective-permute-start(f32[4,512]{1,0:T(4,128)S(1)} %get-tuple-element.29.own_ref), channel_id=1, source_target_pairs={{0,1},{1,2},{2,3},{3,0},{4,5},{5,6},{6,7},{7,4},{8,9},{9,10},{10,1... | collective-permute-start | bytes 24584 | tf_op jit(solution)/shard_map/ppermute | solution.py:372
  59.8 0.0 all-to-all-done.1.pieces_ref
  59.8 0.0 collective-permute-done.9.back_ref
  59.8 3.8 %collective-permute-done.8.far_ref = f32[4,512]{1,0:T(4,128)S(1)} collective-permute-done((f32[4,512]{1,0:T(4,128)S(1)}, f32[4,512]{1,0:T(4,128)S(1)}, u32[]{:S(2)}, u32[]{:S(2)}) %collective-permute-start.8) | collective-permute-done | bytes 8224 | tf_op jit(solution)/shard_map/ppermute | solution.py:372
  63.6 0.1 collective-permute-done.7.near_ref
  63.7 1.3 %collective-permute-start.10 = (bf16[2,2,32,256]{3,2,1,0:T(8,128)(2,1)S(1)}, bf16[2,2,32,256]{3,2,1,0:T(8,128)(2,1)S(1)}, u32[]{:S(2)}, u32[]{:S(2)}) collective-permute-start(bf16[2,2,32,256]{3,2,1,0:T(8,128)(2,1)S(1)} %get-tuple-element.30), channel_id=1, source_target_pairs={{1,0},{2,1},{3,2},{5,4},{6,5},{7,6},{9,8},{10,9},{11,10},{13,12},{... | collective-permute-start | bytes 196616 | tf_op jit(solution)/shard_map/ppermute | solution.py:379
  65.0 4.7 %collective-permute-start.6 = (bf16[2,2,32,256]{3,2,1,0:T(8,128)(2,1)S(1)}, bf16[2,2,32,256]{3,2,1,0:T(8,128)(2,1)S(1)}, u32[]{:S(2)}, u32[]{:S(2)}) collective-permute-start(bf16[2,2,32,256]{3,2,1,0:T(8,128)(2,1)S(1)} %get-tuple-element.40), channel_id=1, source_target_pairs={{0,1},{1,2},{2,3},{4,5},{5,6},{6,7},{8,9},{9,10},{10,11},{12,13},{... | collective-permute-start | bytes 196616 | tf_op jit(solution)/shard_map/ppermute | solution.py:377
  69.7 0.0 copy-done.4
  69.7 10.0 %block.1 = (bf16[2,4,8,16,256]{4,3,2,1,0:T(8,128)(2,1)}, f32[2,2,128,256]{3,2,1,0:T(8,128)S(1)}, bf16[2,2,8,16,256]{4,3,2,1,0:T(8,128)(2,1)}) custom-call(s32[3]{0:T(128)S(1)} %pad_add_fusion.me_ref, bf16[2,4,10,16,512]{4,3,2,1,0:T(8,128)(2,1)S(1)} %get-tuple-element.31.first_ref, f32[4,512]{1,0:T(4,128)S(1)} %get-tuple-element.29.own_ref, ...), custom_call_target="tpu_custom_call" | custom-call | tf_op jit(solution)/shard_map/block/pallas_call | solution.py:382
  79.7 0.0 collective-permute-done.10.high_ref
  79.7 0.0 collective-permute-done.6.low_ref
  79.8 4.8 %cache.1 = bf16[2,4,8,16,256]{4,3,2,1,0:T(8,128)(2,1)} custom-call(s32[2]{0:T(128)S(1)} %copy-done.3, bf16[32,32,256]{2,1,0:T(8,128)(2,1)S(1)} %all-to-all-done.1.pieces_ref, bf16[2,2,32,256]{3,2,1,0:T(8,128)(2,1)S(1)} %collective-permute-done.6.low_ref, ...), custom_call_target="tpu_custom_call", output_to_operand_aliasing={{}: (6, {})} | custom-call | tf_op jit(solution)/shard_map/cache/pallas_call | solution.py:400
  (8 shorter events, 0.1 us)
Async XLA Ops:
  0.6 1.0 %copy-start.1 = (bf16[2,2,8,16,256]{4,3,2,1,0:T(8,128)(2,1)S(1)}, bf16[2,2,8,16,256]{4,3,2,1,0:T(8,128)(2,1)}, u32[]{:S(2)}) copy-start(bf16[2,2,8,16,256]{4,3,2,1,0:T(8,128)(2,1)} %mid_ref.1) | copy-start | bytes 786436
  1.6 0.9 %copy-start.2 = (bf16[2,2,8,16,16]{4,3,2,1,0:T(8,128)(2,1)S(1)}, bf16[2,2,8,16,16]{4,3,2,1,0:T(8,128)(2,1)}, u32[]{:S(2)}) copy-start(bf16[2,2,8,16,16]{4,3,2,1,0:T(8,128)(2,1)} %lat_ref.1) | copy-start | bytes 49156
  2.5 11.1 %copy-start.7 = (bf16[3,3,3,16,256]{4,3,2,1,0:T(8,128)(2,1)S(1)}, bf16[3,3,3,16,256]{4,3,2,1,0:T(8,128)(2,1)}, u32[]{:S(2)}) copy-start(bf16[3,3,3,16,256]{4,3,2,1,0:T(8,128)(2,1)} %param.20) | copy-start | bytes 663556
  2.5 12.6 %copy-start.8 = (f32[256]{0:T(256)S(1)}, f32[256]{0:T(256)}, u32[]{:S(2)}) copy-start(f32[256]{0:T(256)} %param.23) | copy-start | bytes 3076
  2.5 12.6 %copy-start.9 = (f32[256]{0:T(256)S(1)}, f32[256]{0:T(256)}, u32[]{:S(2)}) copy-start(f32[256]{0:T(256)} %param.22) | copy-start | bytes 3076
  2.5 12.6 %copy-start.10 = (f32[256]{0:T(256)S(1)}, f32[256]{0:T(256)}, u32[]{:S(2)}) copy-start(f32[256]{0:T(256)} %param.21) | copy-start | bytes 3076
  2.5 13.3 %copy-start.6 = (bf16[2560,64]{0,1:T(8,128)(2,1)S(1)}, bf16[2560,64]{0,1:T(8,128)(2,1)}, u32[]{:S(2)}) copy-start(bf16[2560,64]{0,1:T(8,128)(2,1)} %param.14) | copy-start | bytes 983044
  3.4 27.3 %all-to-all-start = ((bf16[16,64,256]{2,1,0:T(8,128)(2,1)}), bf16[16,64,256]{2,1,0:T(8,128)(2,1)S(1)}, u32[]{:S(2)}, u32[]{:S(2)}) async-start(bf16[16,64,256]{2,1,0:T(8,128)(2,1)} %pack.1), calls=%async_computation | async-start | bytes 1048576 | tf_op jit(solution)/shard_map/all_to_all | solution.py:319
  13.6 2.6 %copy-start = (bf16[2,4,4,8,2560]{4,3,2,1,0:T(8,128)(2,1)S(1)}, bf16[2,4,4,8,2560]{4,3,2,1,0:T(8,128)(2,1)}, u32[]{:S(2)}) copy-start(bf16[2,4,4,8,2560]{4,3,2,1,0:T(8,128)(2,1)} %param.13) | copy-start | bytes 3932164
  13.6 11.5 %collective-permute-start.1 = (bf16[3,144,256]{2,1,0:T(8,128)(2,1)S(1)}, bf16[3,144,256]{2,1,0:T(8,128)(2,1)S(1)}, u32[]{:S(2)}, u32[]{:S(2)}) collective-permute-start(bf16[3,144,256]{2,1,0:T(8,128)(2,1)S(1)} %bitcast.31), channel_id=1, source_target_pairs={{0,128},{128,0},{1,129},{129,1},{2,130},{130,2},{3,131},{131,3},{4... | collective-permute-start | bytes 663560 | tf_op jit(solution)/shard_map/ppermute | solution.py:321
  15.1 9.9 %collective-permute-start.2 = (f32[3,256]{1,0:T(4,128)S(1)}, f32[3,256]{1,0:T(4,128)S(1)}, u32[]{:S(2)}, u32[]{:S(2)}) collective-permute-start(f32[3,256]{1,0:T(4,128)S(1)} %pad_maximum_fusion), channel_id=1, source_target_pairs={{0,128},{128,0},{1,129},{129,1},{2,130},{130,2},{3,131},{131,3},{4... | collective-permute-start | bytes 9224 | tf_op jit(solution)/shard_map/ppermute | solution.py:321
  16.7 14.0 %copy-start.11 = (f32[64]{0:T(128)S(1)}, f32[64]{0:T(128)}, u32[]{:S(2)}) copy-start(f32[64]{0:T(128)} %param.15) | copy-start | bytes 772
  16.8 15.9 %copy-start.3 = (s32[2]{0:T(128)S(1)}, s32[2]{0:T(128)}, u32[]{:S(2)}) copy-start(s32[2]{0:T(128)} %span_ref.3) | copy-start | bytes 28
  16.8 15.9 %copy-start.5 = (s32[64]{0:T(128)S(1)}, s32[64]{0:T(128)}, u32[]{:S(2)}) copy-start(s32[64]{0:T(128)} %moves_ref.1) | copy-start | bytes 772
  16.8 10.0 %collective-permute-start = (f32[8,16,128]{2,1,0:T(8,128)S(1)}, f32[8,16,128]{2,1,0:T(8,128)S(1)}, u32[]{:S(2)}, u32[]{:S(2)}) collective-permute-start(f32[8,16,128]{2,1,0:T(8,128)S(1)} %head.1.part_ref), channel_id=1, source_target_pairs={{0,128},{128,0},{1,129},{129,1},{2,130},{130,2},{3,131},{131,3},{4... | collective-permute-start | bytes 196616 | tf_op jit(solution)/shard_map/ppermute | solution.py:338
  30.8 1.9 %collective-permute-start.3 = (bf16[16,64,256]{2,1,0:T(8,128)(2,1)S(1)}, bf16[16,64,256]{2,1,0:T(8,128)(2,1)S(1)}, u32[]{:S(2)}, u32[]{:S(2)}) collective-permute-start(bf16[16,64,256]{2,1,0:T(8,128)(2,1)S(1)} %all-to-all-done.got_ref), channel_id=1, source_target_pairs={{0,4},{4,0},{8,12},{12,8},{16,20},{20,16},{24,28},{28,24},{32,36},... | collective-permute-start | bytes 1572872 | tf_op jit(solution)/shard_map/ppermute | solution.py:341
  35.0 34.7 %copy-start.4 = (f32[256]{0:T(256)S(1)}, f32[256]{0:T(256)}, u32[]{:S(2)}) copy-start(f32[256]{0:T(256)} %param.25) | copy-start | bytes 3076
  35.0 24.7 %all-to-all-start.1 = ((bf16[32,32,256]{2,1,0:T(8,128)(2,1)}), bf16[32,32,256]{2,1,0:T(8,128)(2,1)S(1)}, u32[]{:S(2)}, u32[]{:S(2)}) async-start(bf16[32,32,256]{2,1,0:T(8,128)(2,1)} %get-tuple-element.23), calls=%async_computation.1 | async-start | bytes 1048576 | tf_op jit(solution)/shard_map/all_to_all | solution.py:355
  42.5 6.0 %collective-permute-start.5 = (bf16[2,6,16,128]{3,2,1,0:T(8,128)(2,1)S(1)}, bf16[2,6,16,128]{3,2,1,0:T(8,128)(2,1)S(1)}, u32[]{:S(2)}, u32[]{:S(2)}) collective-permute-start(bf16[2,6,16,128]{3,2,1,0:T(8,128)(2,1)S(1)} %get-tuple-element.24.x_ref), channel_id=1, source_target_pairs={{1,0},{2,1},{3,2},{5,4},{6,5},{7,6},{9,8},{10,9},{11,10},{13,12},{... | collective-permute-start | bytes 147464 | tf_op jit(solution)/shard_map/ppermute | solution.py:358
  43.8 6.3 %collective-permute-start.4 = (bf16[2,6,16,128]{3,2,1,0:T(8,128)(2,1)S(1)}, bf16[2,6,16,128]{3,2,1,0:T(8,128)(2,1)S(1)}, u32[]{:S(2)}, u32[]{:S(2)}) collective-permute-start(bf16[2,6,16,128]{3,2,1,0:T(8,128)(2,1)S(1)} %get-tuple-element.24.x_ref), channel_id=1, source_target_pairs={{0,1},{1,2},{2,3},{4,5},{5,6},{6,7},{8,9},{9,10},{10,11},{12,13},{... | collective-permute-start | bytes 147464 | tf_op jit(solution)/shard_map/ppermute | solution.py:357
  54.4 5.4 %collective-permute-start.9 = (f32[4,512]{1,0:T(4,128)S(1)}, f32[4,512]{1,0:T(4,128)S(1)}, u32[]{:S(2)}, u32[]{:S(2)}) collective-permute-start(f32[4,512]{1,0:T(4,128)S(1)} %get-tuple-element.29.own_ref), channel_id=1, source_target_pairs={{0,3},{1,0},{2,1},{3,2},{4,7},{5,4},{6,5},{7,6},{8,11},{9,8},{10,9... | collective-permute-start | bytes 24584 | tf_op jit(solution)/shard_map/ppermute | solution.py:372
  58.5 5.2 %collective-permute-start.8 = (f32[4,512]{1,0:T(4,128)S(1)}, f32[4,512]{1,0:T(4,128)S(1)}, u32[]{:S(2)}, u32[]{:S(2)}) collective-permute-start(f32[4,512]{1,0:T(4,128)S(1)} %get-tuple-element.29.own_ref), channel_id=1, source_target_pairs={{0,2},{1,3},{2,0},{3,1},{4,6},{5,7},{6,4},{7,5},{8,10},{9,11},{10,... | collective-permute-start | bytes 24584 | tf_op jit(solution)/shard_map/ppermute | solution.py:372
  58.8 4.9 %collective-permute-start.7 = (f32[4,512]{1,0:T(4,128)S(1)}, f32[4,512]{1,0:T(4,128)S(1)}, u32[]{:S(2)}, u32[]{:S(2)}) collective-permute-start(f32[4,512]{1,0:T(4,128)S(1)} %get-tuple-element.29.own_ref), channel_id=1, source_target_pairs={{0,1},{1,2},{2,3},{3,0},{4,5},{5,6},{6,7},{7,4},{8,9},{9,10},{10,1... | collective-permute-start | bytes 24584 | tf_op jit(solution)/shard_map/ppermute | solution.py:372
  63.7 16.0 %collective-permute-start.10 = (bf16[2,2,32,256]{3,2,1,0:T(8,128)(2,1)S(1)}, bf16[2,2,32,256]{3,2,1,0:T(8,128)(2,1)S(1)}, u32[]{:S(2)}, u32[]{:S(2)}) collective-permute-start(bf16[2,2,32,256]{3,2,1,0:T(8,128)(2,1)S(1)} %get-tuple-element.30), channel_id=1, source_target_pairs={{1,0},{2,1},{3,2},{5,4},{6,5},{7,6},{9,8},{10,9},{11,10},{13,12},{... | collective-permute-start | bytes 196616 | tf_op jit(solution)/shard_map/ppermute | solution.py:379
  65.0 14.8 %collective-permute-start.6 = (bf16[2,2,32,256]{3,2,1,0:T(8,128)(2,1)S(1)}, bf16[2,2,32,256]{3,2,1,0:T(8,128)(2,1)S(1)}, u32[]{:S(2)}, u32[]{:S(2)}) collective-permute-start(bf16[2,2,32,256]{3,2,1,0:T(8,128)(2,1)S(1)} %get-tuple-element.40), channel_id=1, source_target_pairs={{0,1},{1,2},{2,3},{4,5},{5,6},{6,7},{8,9},{9,10},{10,11},{12,13},{... | collective-permute-start | bytes 196616 | tf_op jit(solution)/shard_map/ppermute | solution.py:377
where the time goes:
time: 85.2 us; the launch traced here: 84.8 us
  starting transfers between devices  38.5 us (45%)
  Pallas kernels  23 us (27%)
  waiting for transfers between devices  19.5 us (23%)
  local copies, waits for them, and re-layouts  2.59 us (3%)
  between operations  1.02 us (1%)
    all_to_all x1, starting transfers between devices, shards(): got = lax.all_to_all(send, 'dec', 0, 0, axis_index_groups=spread)  10.1 us
    pallas_call x1, Pallas kernels, shards(): call(functools.partial(block_kernel, count), 'block', (shape((streams, fr...  9.98 us
    all_to_all x1, starting transfers between devices, shards(): lax.all_to_all(back, ('section', 'dec'), 0, 0, axis_index_groups=gather)  7.42 us
    ppermute x2, waiting for transfers between devices, whole(): other = lax.ppermute(own, 'section', SWAP)  6.77 us
    ppermute x3, starting transfers between devices, shards(): lax.ppermute(stats, 'row', [(i, (i + shift) % bands) for i in range(bands)])  5.38 us
    pallas_call x1, Pallas kernels, shards(): call(cache_kernel, 'cache', shape(decoded.shape, BF16), [SMEM] + [VMEM] *...  4.84 us
    ppermute x1, starting transfers between devices, shards(): low_mid = lax.ppermute(edges[:, :, rows - 1], 'row', down)  4.73 us
    ppermute x1, starting transfers between devices, shards(): low = lax.ppermute(x_in, 'row', down)  4.55 us
  transfers between devices with their start and end apart: 13, of which 8 were waited for; matrix products, arithmetic and copies ran while one was open for 1% of the time, Pallas kernels for 18%

commit v1 on v0

--- a/solution.py
+++ b/solution.py
@@ -63,39 +63,25 @@
     core = dec % 2
     hosts = got_ref.shape[0]
 
-    def place(slot, write):
+    def find(slot, rows, lanes):
         mine = (slot // 2) % 2 == core
-
-        @pl.when(mine)
-        def _():
-            write(got_ref, slot // 4, slot % 2)
-
-        @pl.when(jnp.logical_not(mine))
-        def _():
-            write(twin_ref, slot // 4, slot % 2)
-
+        source = slot // 4
+        return jnp.where(mine, got_ref[source, rows, lanes], twin_ref[source, rows, lanes])
+
+    every = slice(0, got_ref.shape[2])
     for host in range(hosts):
         for k in range(2):
-
-            def write(ref, source, which, host=host, k=k):
-                value = ref[source, pl.ds(pl.multiple_of(which * 16, 16), 16), :]
-                for side in range(2):
-                    send_ref[side * hosts + host, k * 16 : (k + 1) * 16, :] = value
-
-            place(moves_ref[4 * host + 2 * core + k], write)
+            slot = moves_ref[4 * host + 2 * core + k]
+            value = find(slot, pl.ds(pl.multiple_of((slot % 2) * 16, 16), 16), every)
+            for side in range(2):
+                send_ref[side * hosts + host, k * 16 : (k + 1) * 16, :] = value
     for k in range(2):
         live = (span_ref[k] > 0).astype(F32)
-
-        def write_lat(ref, source, which, k=k, live=live):
-            for frame in range(2):
-                lat = ref[
-                    source,
-                    32 + frame * 16 : 48 + frame * 16,
-                    pl.ds(pl.multiple_of(which * 128, 128), 128),
-                ]
-                x_ref[k, frame] = (lat.astype(F32) * live).astype(BF16)
-
-        place(moves_ref[2 * dec + k], write_lat)
+        slot = moves_ref[2 * dec + k]
+        lanes = pl.ds(pl.multiple_of((slot % 2) * 128, 128), 128)
+        for frame in range(2):
+            lat = find(slot, slice(32 + frame * 16, 48 + frame * 16), lanes)
+            x_ref[k, frame] = (lat.astype(F32) * live).astype(BF16)
         for f in range(4):
             latent = part_ref[k * 4 + f] + rest_ref[k * 4 + f] + bias_ref[...]
             x_ref[k, 2 + f] = latent.astype(BF16)
@@ -122,7 +108,7 @@
                 taps[index, r, :, e * 48 : (e + 1) * 48] = value[:, 16 * r : 16 * r + 48]
         return 0
 
-    lax.fori_loop(0, 12, fill, 0)
+    lax.fori_loop(0, 12, fill, 0, unroll=12)
     for k in range(2):
         total = jnp.zeros((640, C), F32) + bias_ref[...]
         for a in range(3):
@@ -160,18 +146,22 @@
 def block_kernel(
     count,
     me_ref,
+    span_ref,
     first_ref,
     own_ref,
     near_ref,
     far_ref,
     back_ref,
+    pieces_ref,
+    low_ref,
+    high_ref,
     vectors_ref,
     bias_ref,
     weight_ref,
     decoded_ref,
-    early_ref,
     cache_ref,
-    taps,
+    taps_0,
+    taps_1,
     weight,
     total,
     sems,
@@ -182,100 +172,70 @@
     ]
     for copy in copies:
         copy.start()
+    taps = (taps_0, taps_1)
+    live = [(span_ref[k] > 0).astype(F32) for k in range(2)]
     sums = group_sum(own_ref[...] + near_ref[...] + far_ref[...] + back_ref[...]) / count
     mean = sums[0:2]
     scale = lax.rsqrt(sums[2:4] - mean * mean + 1e-05) * vectors_ref[1:2]
-    for k in range(2):
-        centre, factor = mean[k : k + 1], scale[k : k + 1]
-
-        def fill(index, _):
-            f, r = index // 10, index % 10
-            value = (first_ref[k, f, r].astype(F32) - centre) * factor + vectors_ref[2:3]
-            value = 0.5 * value * (1.0 + jnp.tanh(0.5 * value))
-            line = row * 8 + r - 1
-            value = jnp.where((line >= 0) & (line < 32), value, 0.0)
-            spread_taps(taps, k * 4 + f, r, value)
+    offset = vectors_ref[2:3]
+    edge = {0: (row > 0).astype(F32), 9: (row < 3).astype(F32)}
+
+    def cached(k, f, r):
+        rows = slice(k * 16, k * 16 + 16)
+        if r == 0:
+            pair = low_ref[0, f, rows], low_ref[1, f, rows]
+        elif r == 9:
+            pair = high_ref[0, f, rows], high_ref[1, f, rows]
+        else:
+            pair = pieces_ref[f * 8 + r - 1, rows], pieces_ref[16 + f * 8 + r - 1, rows]
+        spread_taps(taps[k], f, r, jnp.concatenate(pair, axis=1).astype(F32) * live[k])
+
+    def fresh(k, f, r, border=None):
+        value = (first_ref[k, f, r].astype(F32) - mean[k : k + 1]) * scale[k : k + 1] + offset
+        value = 0.5 * value * (1.0 + jnp.tanh(0.5 * value))
+        if border is not None:
+            value = value * border
+        spread_taps(taps[k], 2 + f, r, value)
+
+    def fill(k):
+        def inner(index, _):
+            fresh(k, index // 8, 1 + index % 8)
             return 0
 
-        lax.fori_loop(0, 40, fill, 0, unroll=2)
+        lax.fori_loop(0, 32, inner, 0, unroll=8)
+        for f in range(4):
+            for r in (0, 9):
+                fresh(k, f, r, edge[r])
+        for f in range(2):
+            for r in range(10):
+                cached(k, f, r)
+
+    def part(k, step):
+        a, b = step // 3, step % 3
+        lhs = taps[k][a : a + 4, b : b + 8].reshape(512, 3 * C)
+        return jnp.dot(lhs, weight[step], preferred_element_type=F32)
+
     start = pl.multiple_of(section * 256, 256)
     for k in range(2):
-        for t in range(4):
-            total[k * 4 + t] = (
-                first_ref[k, t, 1:9, :, pl.ds(start, 256)].astype(F32).reshape(128, 256)
-                + bias_ref[...]
-            )
-        for f in range(2):
-            cache_ref[k, f] = taps[k * 4 + 2 + f, 1:9, :, pl.ds(C + start, 256)]
-    for a in range(3):
-        frames = 2 + a
-        for b in range(3):
-            copies[a * 3 + b].wait()
-            for k in range(2):
-                lhs = taps[k * 4 : k * 4 + frames, b : b + 8].reshape(frames * 128, 3 * C)
-                part = jnp.dot(lhs, weight[a * 3 + b], preferred_element_type=F32)
-                total[k * 4 + 2 - a : k * 4 + 4] += part.reshape(frames, 128, 256)
-    for k in range(2):
-        early_ref[k] = total[k * 4 : k * 4 + 2]
-        for t in range(2, 4):
-            decoded_ref[k, t] = total[k * 4 + t].astype(BF16).reshape(8, 16, 256)
-
-
-def cache_kernel(
-    span_ref,
-    pieces_ref,
-    low_ref,
-    high_ref,
-    early_ref,
-    weight_ref,
-    decoded_ref,
-    out_ref,
-    taps,
-    weight,
-    total,
-    rounded,
-    sems,
-    done,
-):
-    copies = [
-        pltpu.make_async_copy(weight_ref.at[i], weight.at[i], sems.at[i]) for i in range(6)
-    ]
-    for copy in copies:
-        copy.start()
-    for k in range(2):
-        live = (span_ref[k] > 0).astype(F32)
-        rows = slice(k * 16, k * 16 + 16)
-
-        def put(frame, r, left, right):
-            value = jnp.concatenate([left, right], axis=1).astype(F32) * live
-            spread_taps(taps, k * 2 + frame, r, value)
-
-        for frame in range(2):
-            put(frame, 0, low_ref[0, frame, rows], low_ref[1, frame, rows])
-            put(frame, 9, high_ref[0, frame, rows], high_ref[1, frame, rows])
-
-        def fill(index, _):
-            frame, r = index // 8, index % 8
-            put(frame, r + 1, pieces_ref[index, rows], pieces_ref[16 + index, rows])
-            return 0
-
-        lax.fori_loop(0, 16, fill, 0, unroll=2)
-    total[...] = early_ref[...].reshape(total.shape)
-    for a in range(2):
-        frames = 2 - a
-        for b in range(3):
-            copies[a * 3 + b].wait()
-            for k in range(2):
-                lhs = taps[k * 2 + a : k * 2 + 2, b : b + 8].reshape(frames * 128, 3 * C)
-                part = jnp.dot(lhs, weight[a * 3 + b], preferred_element_type=F32)
-                total[k * 2 : k * 2 + frames] += part.reshape(frames, 128, 256)
-    outs = []
-    for k in range(2):
-        rounded[k] = total[k * 2 : k * 2 + 2].astype(BF16).reshape(2, 8, 16, 256)
-        outs.append(pltpu.make_async_copy(rounded.at[k], out_ref.at[k, pl.ds(0, 2)], done.at[k]))
-        outs[k].start()
-    for copy in outs:
-        copy.wait()
+        own = first_ref[k, :, 1:9, :, pl.ds(start, 256)].astype(F32)
+        total[k] = own.reshape(512, 256) + bias_ref[...]
+
+    def finish(k):
+        decoded_ref[k] = total[k].astype(BF16).reshape(4, 8, 16, 256)
+        cache_ref[k] = taps[k][4:6, 1:9, :, pl.ds(C + start, 256)]
+
+    for k in range(2):
+        fill(k)
+    for steps in (range(3), range(3, 9)):
+        for step in steps:
+            copies[step].wait()
+        for k in range(2):
+            value = total[k]
+            for step in steps:
+                value = value + part(k, step)
+            total[k] = value
+    for k in range(2):
+        finish(k)
 
 
 def beside(block):
@@ -313,7 +273,7 @@
     me = jnp.stack([dec, section, row]).astype(jnp.int32)
 
     send = call(
-        pack_kernel, "pack", shape((hosts, 64, part), BF16), [VMEM, VMEM]
+        pack_kernel, "pack", shape((hosts, 64, part), BF16), [VMEM, VMEM], limit=60
     )(lat_cache, mid_cache)
     spread = [[2 * j + c for j in range(hosts)] for c in range(2)]
     got = lax.all_to_all(send, "dec", 0, 0, axis_index_groups=spread)
@@ -379,40 +339,34 @@
     high_mid = lax.ppermute(edge, "row", up)
     taps_weight = mid_weight.reshape(9, 3 * 2 * part, part)
     count = float(frames * rows * bands * cols * (C // GROUPS))
-    decoded, early, new_mid = call(
+    decoded, new_mid = call(
         functools.partial(block_kernel, count),
         "block",
         (
             shape((streams, frames, rows, cols, part), BF16),
-            shape((streams, CACHE, rows * cols, part), F32),
             shape((streams, CACHE, rows, cols, part), BF16),
         ),
-        [SMEM] + [VMEM] * 7 + [ANY],
-        (VMEM, VMEM, VMEM),
-        [
-            pltpu.VMEM((streams * frames, rows + 2, cols, 3 * 2 * part), BF16),
+        [SMEM, SMEM] + [VMEM] * 10 + [ANY],
+        (VMEM, VMEM),
+        [pltpu.VMEM((CACHE + frames, rows + 2, cols, 3 * 2 * part), BF16)] * 2
+        + [
             pltpu.VMEM((9, 3 * 2 * part, part), BF16),
-            pltpu.VMEM((streams * frames, rows * cols, part), F32),
+            pltpu.VMEM((streams, frames * rows * cols, part), F32),
             pltpu.SemaphoreType.DMA((9,)),
         ],
-    )(me, first, stats, *others, vectors, mid_bias.reshape(1, part), taps_weight)
-
-    decoded = call(
-        cache_kernel,
-        "cache",
-        shape(decoded.shape, BF16),
-        [SMEM] + [VMEM] * 4 + [ANY, ANY],
-        ANY,
-        [
-            pltpu.VMEM((streams * CACHE, rows + 2, cols, 3 * 2 * part), BF16),
-            pltpu.VMEM((6, 3 * 2 * part, part), BF16),
-            pltpu.VMEM((streams * CACHE, rows * cols, part), F32),
-            pltpu.VMEM((streams, CACHE, rows, cols, part), BF16),
-            pltpu.SemaphoreType.DMA((6,)),
-            pltpu.SemaphoreType.DMA((2,)),
-        ],
-        {6: 0},
-    )(span_index, pieces, low_mid, high_mid, early, taps_weight, decoded)
+    )(
+        me,
+        span_index,
+        first,
+        stats,
+        *others,
+        pieces,
+        low_mid,
+        high_mid,
+        vectors,
+        mid_bias.reshape(1, part),
+        taps_weight,
+    )
     return (decoded, new_lat, new_mid)
 
 

time: 85.2 us -> 80.8 us (0.948)
  Pallas kernels: 23 us -> 18.1 us
  local copies, waits for them, and re-layouts: 2.59 us -> 0.75 us
  waiting for transfers between devices: 19.5 us -> 21.1 us
    pallas_call x2 -> x1, Pallas kernels: 5.74 us -> 2.03 us  [shards(): call(pack_kernel, 'pack', shape((hosts, 64, part), BF16), [VMEM, VMEM], l...]
    pallas_call x1, Pallas kernels: 4.34 us -> 2.33 us  [shards(): call(first_kernel, 'first', (shape((streams, frames, rows + 2, cols, 2 *...]
    unnamed x24 -> x20, local copies, waits for them, and re-layouts: 1.89 us -> 0.05 us
    ppermute x1, waiting for transfers between devices: 0.01 us -> 1.58 us  [shards(): low_mid = lax.ppermute(edges[:, :, rows - 1], 'row', down)]
    pallas_call x1, Pallas kernels: 9.98 us -> 11.3 us  [shards(): call(functools.partial(block_kernel, count), 'block', (shape((streams, fr...]
  transfers between devices with their start and end apart: 13 -> 13, of which waited for: 8 -> 11; matrix products, arithmetic and copies ran while one was open for 1% -> 1% of each run, Pallas kernels for 18% -> 4%
where the time goes in v1:
time: 80.8 us; the launch traced here: 79.6 us
  starting transfers between devices  38.5 us (48%)
  waiting for transfers between devices  21.1 us (26%)
  Pallas kernels  18.1 us (22%)
  between operations  1.01 us (1%)
    pallas_call x1, Pallas kernels, shards(): call(functools.partial(block_kernel, count), 'block', (shape((streams, fr...  11.3 us
    all_to_all x1, starting transfers between devices, shards(): got = lax.all_to_all(send, 'dec', 0, 0, axis_index_groups=spread)  10.1 us
    all_to_all x1, starting transfers between devices, shards(): lax.all_to_all(back, ('section', 'dec'), 0, 0, axis_index_groups=gather)  7.42 us
    ppermute x2, waiting for transfers between devices, whole(): other = lax.ppermute(own, 'section', SWAP)  6.76 us
    ppermute x3, starting transfers between devices, shards(): lax.ppermute(stats, 'row', [(i, (i + shift) % bands) for i in range(bands)])  5.37 us
    ppermute x1, starting transfers between devices, shards(): low_mid = lax.ppermute(edges[:, :, rows - 1], 'row', down)  4.73 us
    ppermute x1, starting transfers between devices, shards(): low = lax.ppermute(x_in, 'row', down)  4.55 us
    all_to_all x1, waiting for transfers between devices, shards(): got = lax.all_to_all(send, 'dec', 0, 0, axis_index_groups=spread)  4 us
  transfers between devices with their start and end apart: 13, of which 11 were waited for; matrix products, arithmetic and copies ran while one was open for 1% of the time, Pallas kernels for 4%

profile of v1, /device:TPU:2, one launch (start us, length us, event | category | flops | bytes accessed | tf_op | source)
XLA Modules:
  0.0 79.6 jit_solution(3399486620050060483)
XLA Ops:
  0.6 0.0 copy-start.5
  0.6 0.0 copy-start.6
  0.7 0.0 copy-start.7
  0.7 0.0 copy-start.8
  0.7 0.0 copy-start.4
  0.7 2.0 %pack.1 = bf16[16,64,256]{2,1,0:T(8,128)(2,1)} custom-call(bf16[2,2,8,16,16]{4,3,2,1,0:T(8,128)(2,1)} %lat_ref.1, bf16[2,2,8,16,256]{4,3,2,1,0:T(8,128)(2,1)} %mid_ref.1), custom_call_target="tpu_custom_call" | custom-call | tf_op jit(solution)/shard_map/pack/pallas_call | solution.py:275
  2.7 10.1 %all-to-all-start = ((bf16[16,64,256]{2,1,0:T(8,128)(2,1)}), bf16[16,64,256]{2,1,0:T(8,128)(2,1)S(1)}, u32[]{:S(2)}, u32[]{:S(2)}) async-start(bf16[16,64,256]{2,1,0:T(8,128)(2,1)} %pack.1), calls=%async_computation | async-start | bytes 1048576 | tf_op jit(solution)/shard_map/all_to_all | solution.py:279
  12.9 0.0 copy-start
  12.9 0.0 copy-done.5
  12.9 1.5 %collective-permute-start.1 = (bf16[3,144,256]{2,1,0:T(8,128)(2,1)S(1)}, bf16[3,144,256]{2,1,0:T(8,128)(2,1)S(1)}, u32[]{:S(2)}, u32[]{:S(2)}) collective-permute-start(bf16[3,144,256]{2,1,0:T(8,128)(2,1)S(1)} %bitcast.30), channel_id=1, source_target_pairs={{0,128},{128,0},{1,129},{129,1},{2,130},{130,2},{3,131},{131,3},{4... | collective-permute-start | bytes 663560 | tf_op jit(solution)/shard_map/ppermute | solution.py:281
  14.4 0.0 copy-done.6
  14.4 0.0 copy-done.7
  14.4 0.0 copy-done.8
  14.4 0.7 collective-permute-start.2
  15.1 0.0 copy-done.4
  15.1 0.3 copy.25.weight_ref
  15.5 0.0 copy-done
  15.5 0.6 head.1.part_ref
  16.1 0.0 copy-start.9
  16.1 0.0 copy-start.1
  16.1 0.0 copy-start.3
  16.1 1.5 %collective-permute-start = (f32[8,16,128]{2,1,0:T(8,128)S(1)}, f32[8,16,128]{2,1,0:T(8,128)S(1)}, u32[]{:S(2)}, u32[]{:S(2)}) collective-permute-start(f32[8,16,128]{2,1,0:T(8,128)S(1)} %head.1.part_ref), channel_id=1, source_target_pairs={{0,128},{128,0},{1,129},{129,1},{2,130},{130,2},{3,131},{131,3},{4... | collective-permute-start | bytes 196616 | tf_op jit(solution)/shard_map/ppermute | solution.py:298
  17.6 6.8 %collective-permute-done.2 = f32[3,256]{1,0:T(4,128)S(1)} collective-permute-done((f32[3,256]{1,0:T(4,128)S(1)}, f32[3,256]{1,0:T(4,128)S(1)}, u32[]{:S(2)}, u32[]{:S(2)}) %collective-permute-start.2) | collective-permute-done | bytes 3104 | tf_op jit(solution)/shard_map/ppermute | solution.py:281
  24.4 0.0 collective-permute-done.1
  24.4 0.1 maximum_select_fusion
  24.5 0.1 pad.4.weight_ref
  24.6 1.5 %collective-permute-done.rest_ref = f32[8,16,128]{2,1,0:T(8,128)S(1)} collective-permute-done((f32[8,16,128]{2,1,0:T(8,128)S(1)}, f32[8,16,128]{2,1,0:T(8,128)S(1)}, u32[]{:S(2)}, u32[]{:S(2)}) %collective-permute-start) | collective-permute-done | bytes 65568 | tf_op jit(solution)/shard_map/ppermute | solution.py:298
  26.1 4.0 %all-to-all-done.got_ref = bf16[16,64,256]{2,1,0:T(8,128)(2,1)S(1)} async-done(((bf16[16,64,256]{2,1,0:T(8,128)(2,1)}), bf16[16,64,256]{2,1,0:T(8,128)(2,1)S(1)}, u32[]{:S(2)}, u32[]{:S(2)}) %all-to-all-start) | async-done | bytes 524320 | tf_op jit(solution)/shard_map/all_to_all | solution.py:279
  30.1 0.0 collective-permute-start.3
  30.1 0.0 copy-done.9
  30.1 0.1 reshape.39
  30.1 0.1 broadcast_in_dim.7
  30.2 0.1 reshape.40.bias_ref
  30.3 0.1 pad_add_fusion.me_ref
  30.4 1.6 %collective-permute-done.3.twin_ref = bf16[16,64,256]{2,1,0:T(8,128)(2,1)S(1)} collective-permute-done((bf16[16,64,256]{2,1,0:T(8,128)(2,1)S(1)}, bf16[16,64,256]{2,1,0:T(8,128)(2,1)S(1)}, u32[]{:S(2)}, u32[]{:S(2)}) %collective-permute-start.3) | collective-permute-done | bytes 524320 | tf_op jit(solution)/shard_map/ppermute | solution.py:301
  32.0 0.0 copy-done.1
  32.0 0.0 copy-done.3
  32.0 1.8 %pick.1 = (bf16[32,32,256]{2,1,0:T(8,128)(2,1)}, bf16[2,6,16,128]{3,2,1,0:T(8,128)(2,1)S(1)}) custom-call(s32[3]{0:T(128)S(1)} %pad_add_fusion.me_ref, s32[64]{0:T(128)S(1)} %copy-done.3, s32[2]{0:T(128)S(1)} %copy-done.1, bf16[16,64,256]{2,1,0:T(8,128)(2,1)S(1)} %all-to-all-done.got_ref, bf16[16,64,256]{2,1,0:T(8,128)(2,1)S(1)} %collective-permute-done.3.twin_ref, ...), custom_call_target="tpu_custom_call" | custom-call | tf_op jit(solution)/shard_map/pick/pallas_call | solution.py:302
  33.8 0.0 copy-start.2
  33.8 7.4 %all-to-all-start.1 = ((bf16[32,32,256]{2,1,0:T(8,128)(2,1)}), bf16[32,32,256]{2,1,0:T(8,128)(2,1)S(1)}, u32[]{:S(2)}, u32[]{:S(2)}) async-start(bf16[32,32,256]{2,1,0:T(8,128)(2,1)} %get-tuple-element.27), calls=%async_computation.1 | async-start | bytes 1048576 | tf_op jit(solution)/shard_map/all_to_all | solution.py:315
  41.2 1.3 %collective-permute-start.5 = (bf16[2,6,16,128]{3,2,1,0:T(8,128)(2,1)S(1)}, bf16[2,6,16,128]{3,2,1,0:T(8,128)(2,1)S(1)}, u32[]{:S(2)}, u32[]{:S(2)}) collective-permute-start(bf16[2,6,16,128]{3,2,1,0:T(8,128)(2,1)S(1)} %get-tuple-element.22.x_ref), channel_id=1, source_target_pairs={{1,0},{2,1},{3,2},{5,4},{6,5},{7,6},{9,8},{10,9},{11,10},{13,12},{... | collective-permute-start | bytes 147464 | tf_op jit(solution)/shard_map/ppermute | solution.py:318
  42.5 4.5 %collective-permute-start.4 = (bf16[2,6,16,128]{3,2,1,0:T(8,128)(2,1)S(1)}, bf16[2,6,16,128]{3,2,1,0:T(8,128)(2,1)S(1)}, u32[]{:S(2)}, u32[]{:S(2)}) collective-permute-start(bf16[2,6,16,128]{3,2,1,0:T(8,128)(2,1)S(1)} %get-tuple-element.22.x_ref), channel_id=1, source_target_pairs={{0,1},{1,2},{2,3},{4,5},{5,6},{6,7},{8,9},{9,10},{10,11},{12,13},{... | collective-permute-start | bytes 147464 | tf_op jit(solution)/shard_map/ppermute | solution.py:317
  47.1 0.1 collective-permute-done.5.high_ref
  47.2 1.6 %collective-permute-done.4.low_ref = bf16[2,6,16,128]{3,2,1,0:T(8,128)(2,1)S(1)} collective-permute-done((bf16[2,6,16,128]{3,2,1,0:T(8,128)(2,1)S(1)}, bf16[2,6,16,128]{3,2,1,0:T(8,128)(2,1)S(1)}, u32[]{:S(2)}, u32[]{:S(2)}) %collective-permute-start.4) | collective-permute-done | bytes 49184 | tf_op jit(solution)/shard_map/ppermute | solution.py:317
  48.8 2.3 %first.1 = (bf16[2,4,10,16,512]{4,3,2,1,0:T(8,128)(2,1)S(1)}, f32[4,512]{1,0:T(4,128)S(1)}, bf16[2,2,8,16,16]{4,3,2,1,0:T(8,128)(2,1)}) custom-call(bf16[2,6,16,128]{3,2,1,0:T(8,128)(2,1)S(1)} %get-tuple-element.22.x_ref, bf16[2,6,16,128]{3,2,1,0:T(8,128)(2,1)S(1)} %collective-permute-done.4.low_ref, ...), custom_call_target="tpu_custom_call" | custom-call | tf_op jit(solution)/shard_map/first/pallas_call | solution.py:319
  51.1 4.1 %collective-permute-start.8 = (f32[4,512]{1,0:T(4,128)S(1)}, f32[4,512]{1,0:T(4,128)S(1)}, u32[]{:S(2)}, u32[]{:S(2)}) collective-permute-start(f32[4,512]{1,0:T(4,128)S(1)} %get-tuple-element.26.own_ref), channel_id=1, source_target_pairs={{0,3},{1,0},{2,1},{3,2},{4,7},{5,4},{6,5},{7,6},{8,11},{9,8},{10,9... | collective-permute-start | bytes 24584 | tf_op jit(solution)/shard_map/ppermute | solution.py:332
  55.2 0.3 collective-permute-start.7
  55.5 1.0 %collective-permute-start.6 = (f32[4,512]{1,0:T(4,128)S(1)}, f32[4,512]{1,0:T(4,128)S(1)}, u32[]{:S(2)}, u32[]{:S(2)}) collective-permute-start(f32[4,512]{1,0:T(4,128)S(1)} %get-tuple-element.26.own_ref), channel_id=1, source_target_pairs={{0,1},{1,2},{2,3},{3,0},{4,5},{5,6},{6,7},{7,4},{8,9},{9,10},{10,1... | collective-permute-start | bytes 24584 | tf_op jit(solution)/shard_map/ppermute | solution.py:332
  56.5 0.7 all-to-all-done.1.pieces_ref
  57.3 0.0 collective-permute-done.8.back_ref
  57.3 3.1 %collective-permute-done.7.far_ref = f32[4,512]{1,0:T(4,128)S(1)} collective-permute-done((f32[4,512]{1,0:T(4,128)S(1)}, f32[4,512]{1,0:T(4,128)S(1)}, u32[]{:S(2)}, u32[]{:S(2)}) %collective-permute-start.7) | collective-permute-done | bytes 8224 | tf_op jit(solution)/shard_map/ppermute | solution.py:332
  60.3 0.1 collective-permute-done.6.near_ref
  60.4 1.3 %collective-permute-start.10 = (bf16[2,2,32,256]{3,2,1,0:T(8,128)(2,1)S(1)}, bf16[2,2,32,256]{3,2,1,0:T(8,128)(2,1)S(1)}, u32[]{:S(2)}, u32[]{:S(2)}) collective-permute-start(bf16[2,2,32,256]{3,2,1,0:T(8,128)(2,1)S(1)} %get-tuple-element.33), channel_id=1, source_target_pairs={{1,0},{2,1},{3,2},{5,4},{6,5},{7,6},{9,8},{10,9},{11,10},{13,12},{... | collective-permute-start | bytes 196616 | tf_op jit(solution)/shard_map/ppermute | solution.py:339
  61.7 4.7 %collective-permute-start.9 = (bf16[2,2,32,256]{3,2,1,0:T(8,128)(2,1)S(1)}, bf16[2,2,32,256]{3,2,1,0:T(8,128)(2,1)S(1)}, u32[]{:S(2)}, u32[]{:S(2)}) collective-permute-start(bf16[2,2,32,256]{3,2,1,0:T(8,128)(2,1)S(1)} %get-tuple-element.37), channel_id=1, source_target_pairs={{0,1},{1,2},{2,3},{4,5},{5,6},{6,7},{8,9},{9,10},{10,11},{12,13},{... | collective-permute-start | bytes 196616 | tf_op jit(solution)/shard_map/ppermute | solution.py:337
  66.5 0.1 collective-permute-done.10.high_ref
  66.6 1.6 %collective-permute-done.9.low_ref = bf16[2,2,32,256]{3,2,1,0:T(8,128)(2,1)S(1)} collective-permute-done((bf16[2,2,32,256]{3,2,1,0:T(8,128)(2,1)S(1)}, bf16[2,2,32,256]{3,2,1,0:T(8,128)(2,1)S(1)}, u32[]{:S(2)}, u32[]{:S(2)}) %collective-permute-start.9) | collective-permute-done | bytes 65568 | tf_op jit(solution)/shard_map/ppermute | solution.py:337
  68.2 0.0 copy-done.2
  68.2 11.3 %block.1 = (bf16[2,4,8,16,256]{4,3,2,1,0:T(8,128)(2,1)}, bf16[2,2,8,16,256]{4,3,2,1,0:T(8,128)(2,1)}) custom-call(s32[3]{0:T(128)S(1)} %pad_add_fusion.me_ref, s32[2]{0:T(128)S(1)} %copy-done.1, bf16[2,4,10,16,512]{4,3,2,1,0:T(8,128)(2,1)S(1)} %get-tuple-element.25.first_ref, f32[4,512]{1,0:T(4,128)S(1)} %get-tuple-element.26.own_ref, ...), custom_call_target="tpu_custom_call" | custom-call | tf_op jit(solution)/shard_map/block/pallas_call | solution.py:342
  (8 shorter events, 0.1 us)
Async XLA Ops:
  0.6 12.2 %copy-start.5 = (bf16[3,3,3,16,256]{4,3,2,1,0:T(8,128)(2,1)S(1)}, bf16[3,3,3,16,256]{4,3,2,1,0:T(8,128)(2,1)}, u32[]{:S(2)}) copy-start(bf16[3,3,3,16,256]{4,3,2,1,0:T(8,128)(2,1)} %param.20) | copy-start | bytes 663556
  0.6 13.8 %copy-start.6 = (f32[256]{0:T(256)S(1)}, f32[256]{0:T(256)}, u32[]{:S(2)}) copy-start(f32[256]{0:T(256)} %param.23) | copy-start | bytes 3076
  0.7 13.8 %copy-start.7 = (f32[256]{0:T(256)S(1)}, f32[256]{0:T(256)}, u32[]{:S(2)}) copy-start(f32[256]{0:T(256)} %param.22) | copy-start | bytes 3076
  0.7 13.8 %copy-start.8 = (f32[256]{0:T(256)S(1)}, f32[256]{0:T(256)}, u32[]{:S(2)}) copy-start(f32[256]{0:T(256)} %param.21) | copy-start | bytes 3076
  0.7 14.4 %copy-start.4 = (bf16[2560,64]{0,1:T(8,128)(2,1)S(1)}, bf16[2560,64]{0,1:T(8,128)(2,1)}, u32[]{:S(2)}) copy-start(bf16[2560,64]{0,1:T(8,128)(2,1)} %param.14) | copy-start | bytes 983044
  2.7 27.3 %all-to-all-start = ((bf16[16,64,256]{2,1,0:T(8,128)(2,1)}), bf16[16,64,256]{2,1,0:T(8,128)(2,1)S(1)}, u32[]{:S(2)}, u32[]{:S(2)}) async-start(bf16[16,64,256]{2,1,0:T(8,128)(2,1)} %pack.1), calls=%async_computation | async-start | bytes 1048576 | tf_op jit(solution)/shard_map/all_to_all | solution.py:279
  12.9 2.6 %copy-start = (bf16[2,4,4,8,2560]{4,3,2,1,0:T(8,128)(2,1)S(1)}, bf16[2,4,4,8,2560]{4,3,2,1,0:T(8,128)(2,1)}, u32[]{:S(2)}) copy-start(bf16[2,4,4,8,2560]{4,3,2,1,0:T(8,128)(2,1)} %param.13) | copy-start | bytes 3932164
  12.9 11.5 %collective-permute-start.1 = (bf16[3,144,256]{2,1,0:T(8,128)(2,1)S(1)}, bf16[3,144,256]{2,1,0:T(8,128)(2,1)S(1)}, u32[]{:S(2)}, u32[]{:S(2)}) collective-permute-start(bf16[3,144,256]{2,1,0:T(8,128)(2,1)S(1)} %bitcast.30), channel_id=1, source_target_pairs={{0,128},{128,0},{1,129},{129,1},{2,130},{130,2},{3,131},{131,3},{4... | collective-permute-start | bytes 663560 | tf_op jit(solution)/shard_map/ppermute | solution.py:281
  14.4 9.9 %collective-permute-start.2 = (f32[3,256]{1,0:T(4,128)S(1)}, f32[3,256]{1,0:T(4,128)S(1)}, u32[]{:S(2)}, u32[]{:S(2)}) collective-permute-start(f32[3,256]{1,0:T(4,128)S(1)} %pad_maximum_fusion), channel_id=1, source_target_pairs={{0,128},{128,0},{1,129},{129,1},{2,130},{130,2},{3,131},{131,3},{4... | collective-permute-start | bytes 9224 | tf_op jit(solution)/shard_map/ppermute | solution.py:281
  16.1 14.0 %copy-start.9 = (f32[64]{0:T(128)S(1)}, f32[64]{0:T(128)}, u32[]{:S(2)}) copy-start(f32[64]{0:T(128)} %param.15) | copy-start | bytes 772
  16.1 15.9 %copy-start.1 = (s32[2]{0:T(128)S(1)}, s32[2]{0:T(128)}, u32[]{:S(2)}) copy-start(s32[2]{0:T(128)} %span_ref.3) | copy-start | bytes 28
  16.1 15.9 %copy-start.3 = (s32[64]{0:T(128)S(1)}, s32[64]{0:T(128)}, u32[]{:S(2)}) copy-start(s32[64]{0:T(128)} %moves_ref.1) | copy-start | bytes 772
  16.1 10.0 %collective-permute-start = (f32[8,16,128]{2,1,0:T(8,128)S(1)}, f32[8,16,128]{2,1,0:T(8,128)S(1)}, u32[]{:S(2)}, u32[]{:S(2)}) collective-permute-start(f32[8,16,128]{2,1,0:T(8,128)S(1)} %head.1.part_ref), channel_id=1, source_target_pairs={{0,128},{128,0},{1,129},{129,1},{2,130},{130,2},{3,131},{131,3},{4... | collective-permute-start | bytes 196616 | tf_op jit(solution)/shard_map/ppermute | solution.py:298
  30.1 1.9 %collective-permute-start.3 = (bf16[16,64,256]{2,1,0:T(8,128)(2,1)S(1)}, bf16[16,64,256]{2,1,0:T(8,128)(2,1)S(1)}, u32[]{:S(2)}, u32[]{:S(2)}) collective-permute-start(bf16[16,64,256]{2,1,0:T(8,128)(2,1)S(1)} %all-to-all-done.got_ref), channel_id=1, source_target_pairs={{0,4},{4,0},{8,12},{12,8},{16,20},{20,16},{24,28},{28,24},{32,36},... | collective-permute-start | bytes 1572872 | tf_op jit(solution)/shard_map/ppermute | solution.py:301
  33.8 34.4 %copy-start.2 = (f32[256]{0:T(256)S(1)}, f32[256]{0:T(256)}, u32[]{:S(2)}) copy-start(f32[256]{0:T(256)} %param.25) | copy-start | bytes 3076
  33.8 23.5 %all-to-all-start.1 = ((bf16[32,32,256]{2,1,0:T(8,128)(2,1)}), bf16[32,32,256]{2,1,0:T(8,128)(2,1)S(1)}, u32[]{:S(2)}, u32[]{:S(2)}) async-start(bf16[32,32,256]{2,1,0:T(8,128)(2,1)} %get-tuple-element.27), calls=%async_computation.1 | async-start | bytes 1048576 | tf_op jit(solution)/shard_map/all_to_all | solution.py:315
  41.2 6.0 %collective-permute-start.5 = (bf16[2,6,16,128]{3,2,1,0:T(8,128)(2,1)S(1)}, bf16[2,6,16,128]{3,2,1,0:T(8,128)(2,1)S(1)}, u32[]{:S(2)}, u32[]{:S(2)}) collective-permute-start(bf16[2,6,16,128]{3,2,1,0:T(8,128)(2,1)S(1)} %get-tuple-element.22.x_ref), channel_id=1, source_target_pairs={{1,0},{2,1},{3,2},{5,4},{6,5},{7,6},{9,8},{10,9},{11,10},{13,12},{... | collective-permute-start | bytes 147464 | tf_op jit(solution)/shard_map/ppermute | solution.py:318
  42.5 6.3 %collective-permute-start.4 = (bf16[2,6,16,128]{3,2,1,0:T(8,128)(2,1)S(1)}, bf16[2,6,16,128]{3,2,1,0:T(8,128)(2,1)S(1)}, u32[]{:S(2)}, u32[]{:S(2)}) collective-permute-start(bf16[2,6,16,128]{3,2,1,0:T(8,128)(2,1)S(1)} %get-tuple-element.22.x_ref), channel_id=1, source_target_pairs={{0,1},{1,2},{2,3},{4,5},{5,6},{6,7},{8,9},{9,10},{10,11},{12,13},{... | collective-permute-start | bytes 147464 | tf_op jit(solution)/shard_map/ppermute | solution.py:317
  51.1 6.1 %collective-permute-start.8 = (f32[4,512]{1,0:T(4,128)S(1)}, f32[4,512]{1,0:T(4,128)S(1)}, u32[]{:S(2)}, u32[]{:S(2)}) collective-permute-start(f32[4,512]{1,0:T(4,128)S(1)} %get-tuple-element.26.own_ref), channel_id=1, source_target_pairs={{0,3},{1,0},{2,1},{3,2},{4,7},{5,4},{6,5},{7,6},{8,11},{9,8},{10,9... | collective-permute-start | bytes 24584 | tf_op jit(solution)/shard_map/ppermute | solution.py:332
  55.2 5.2 %collective-permute-start.7 = (f32[4,512]{1,0:T(4,128)S(1)}, f32[4,512]{1,0:T(4,128)S(1)}, u32[]{:S(2)}, u32[]{:S(2)}) collective-permute-start(f32[4,512]{1,0:T(4,128)S(1)} %get-tuple-element.26.own_ref), channel_id=1, source_target_pairs={{0,2},{1,3},{2,0},{3,1},{4,6},{5,7},{6,4},{7,5},{8,10},{9,11},{10,... | collective-permute-start | bytes 24584 | tf_op jit(solution)/shard_map/ppermute | solution.py:332
  55.5 4.9 %collective-permute-start.6 = (f32[4,512]{1,0:T(4,128)S(1)}, f32[4,512]{1,0:T(4,128)S(1)}, u32[]{:S(2)}, u32[]{:S(2)}) collective-permute-start(f32[4,512]{1,0:T(4,128)S(1)} %get-tuple-element.26.own_ref), channel_id=1, source_target_pairs={{0,1},{1,2},{2,3},{3,0},{4,5},{5,6},{6,7},{7,4},{8,9},{9,10},{10,1... | collective-permute-start | bytes 24584 | tf_op jit(solution)/shard_map/ppermute | solution.py:332
  60.4 6.1 %collective-permute-start.10 = (bf16[2,2,32,256]{3,2,1,0:T(8,128)(2,1)S(1)}, bf16[2,2,32,256]{3,2,1,0:T(8,128)(2,1)S(1)}, u32[]{:S(2)}, u32[]{:S(2)}) collective-permute-start(bf16[2,2,32,256]{3,2,1,0:T(8,128)(2,1)S(1)} %get-tuple-element.33), channel_id=1, source_target_pairs={{1,0},{2,1},{3,2},{5,4},{6,5},{7,6},{9,8},{10,9},{11,10},{13,12},{... | collective-permute-start | bytes 196616 | tf_op jit(solution)/shard_map/ppermute | solution.py:339
  61.7 6.4 %collective-permute-start.9 = (bf16[2,2,32,256]{3,2,1,0:T(8,128)(2,1)S(1)}, bf16[2,2,32,256]{3,2,1,0:T(8,128)(2,1)S(1)}, u32[]{:S(2)}, u32[]{:S(2)}) collective-permute-start(bf16[2,2,32,256]{3,2,1,0:T(8,128)(2,1)S(1)} %get-tuple-element.37), channel_id=1, source_target_pairs={{0,1},{1,2},{2,3},{4,5},{5,6},{6,7},{8,9},{9,10},{10,11},{12,13},{... | collective-permute-start | bytes 196616 | tf_op jit(solution)/shard_map/ppermute | solution.py:337

commit v2 on v1

--- a/solution.py
+++ b/solution.py
@@ -94,14 +94,17 @@
     return jnp.where(line == edge, 0.0, moved)
 
 
-def first_kernel(x_ref, low_ref, high_ref, weight_ref, bias_ref, first_ref, stats_ref, lat_ref, taps):
+def first_kernel(me_ref, x_ref, low_ref, high_ref, weight_ref, bias_ref, first_ref, stats_ref, lat_ref, taps):
     taps[...] = jnp.zeros_like(taps)
+
+    above = (me_ref[2] > 0).astype(F32)
+    below = (me_ref[2] < 3).astype(F32)
 
     def fill(index, _):
         k, f = index // 6, index % 6
-        wide = jnp.concatenate(
-            [low_ref[k, f][:, 96:], x_ref[k, f], high_ref[k, f][:, :32]], axis=1
-        ).astype(F32)
+        low = low_ref[k, f].astype(F32)[:, 96:] * above
+        high = high_ref[k, f].astype(F32)[:, :32] * below
+        wide = jnp.concatenate([low, x_ref[k, f].astype(F32), high], axis=1)
         for e, value in enumerate((shifted(wide, 1), wide, shifted(wide, -1))):
             value = value.astype(BF16)
             for r in range(10):
@@ -188,7 +191,8 @@
             pair = high_ref[0, f, rows], high_ref[1, f, rows]
         else:
             pair = pieces_ref[f * 8 + r - 1, rows], pieces_ref[16 + f * 8 + r - 1, rows]
-        spread_taps(taps[k], f, r, jnp.concatenate(pair, axis=1).astype(F32) * live[k])
+        inside = live[k] * edge[r] if r in (0, 9) else live[k]
+        spread_taps(taps[k], f, r, jnp.concatenate(pair, axis=1).astype(F32) * inside)
 
     def fresh(k, f, r, border=None):
         value = (first_ref[k, f, r].astype(F32) - mean[k : k + 1]) * scale[k : k + 1] + offset
@@ -238,10 +242,10 @@
         finish(k)
 
 
-def beside(block):
+def beside():
     count = lax.axis_size("row")
-    down = [(i, i + 1) for i in range(count - 1)]
-    up = [(i + 1, i) for i in range(count - 1)]
+    down = [(i, (i + 1) % count) for i in range(count)]
+    up = [((i + 1) % count, i) for i in range(count)]
     return down, up
 
 
@@ -268,7 +272,7 @@
     row = lax.axis_index("row")
     bands = lax.axis_size("row")
     hosts = lax.axis_size("dec") // 2
-    down, up = beside(None)
+    down, up = beside()
     shape = jax.ShapeDtypeStruct
     me = jnp.stack([dec, section, row]).astype(jnp.int32)
 
@@ -324,10 +328,10 @@
             shape((4, 2 * part), F32),
             shape((streams, CACHE, rows, cols, CZ), BF16),
         ),
-        [VMEM] * 5,
+        [SMEM] + [VMEM] * 5,
         (VMEM, VMEM, VMEM),
         [pltpu.VMEM((streams * (CACHE + frames), rows + 2, cols, 256), BF16)],
-    )(x_in, low, high, in_weight, vectors[0:1])
+    )(me, x_in, low, high, in_weight, vectors[0:1])
     others = [
         lax.ppermute(stats, "row", [(i, (i + shift) % bands) for i in range(bands)])
         for shift in range(1, bands)

time: 80.8 us -> 79.3 us (0.981)
  starting transfers between devices: 38.5 us -> 28.5 us
  waiting for transfers between devices: 21.1 us -> 28.8 us
    ppermute x1, starting transfers between devices: 4.73 us -> 0.01 us  [shards(): low_mid = lax.ppermute(edges[:, :, rows - 1], 'row', down)]
    ppermute x1, starting transfers between devices: 4.55 us -> 0.01 us  [shards(): low = lax.ppermute(x_in, 'row', down)]
    ppermute x3, starting transfers between devices: 5.37 us -> 2.03 us  [shards(): lax.ppermute(stats, 'row', [(i, (i + shift) % bands) for i in range(bands)])]
    ppermute x1, waiting for transfers between devices: 0.12 us -> 2.15 us  [shards(): high_mid = lax.ppermute(edge, 'row', up)]
    all_to_all x1, waiting for transfers between devices: 0.74 us -> 2.71 us  [shards(): lax.all_to_all(back, ('section', 'dec'), 0, 0, axis_index_groups=gather)]
    ppermute x1, waiting for transfers between devices: 1.6 us -> 3.55 us  [shards(): low = lax.ppermute(x_in, 'row', down)]
    ppermute x1, starting transfers between devices: 1.29 us -> 3.09 us  [shards(): high = lax.ppermute(x_in, 'row', up)]
    ppermute x1, waiting for transfers between devices: 1.58 us -> 3.32 us  [shards(): low_mid = lax.ppermute(edges[:, :, rows - 1], 'row', down)]
where the time goes in v2:
time: 79.3 us; the launch traced here: 77.9 us
  waiting for transfers between devices  28.8 us (36%)
  starting transfers between devices  28.5 us (36%)
  Pallas kernels  18.6 us (23%)
  between operations  0.98 us (1%)
    pallas_call x1, Pallas kernels, shards(): call(functools.partial(block_kernel, count), 'block', (shape((streams, fr...  11.3 us
    all_to_all x1, starting transfers between devices, shards(): got = lax.all_to_all(send, 'dec', 0, 0, axis_index_groups=spread)  10.1 us
    all_to_all x1, starting transfers between devices, shards(): lax.all_to_all(back, ('section', 'dec'), 0, 0, axis_index_groups=gather)  7.42 us
    ppermute x2, waiting for transfers between devices, whole(): other = lax.ppermute(own, 'section', SWAP)  6.76 us
    all_to_all x1, waiting for transfers between devices, shards(): got = lax.all_to_all(send, 'dec', 0, 0, axis_index_groups=spread)  4 us
    ppermute x1, waiting for transfers between devices, shards(): low = lax.ppermute(x_in, 'row', down)  3.55 us
    ppermute x1, waiting for transfers between devices, shards(): low_mid = lax.ppermute(edges[:, :, rows - 1], 'row', down)  3.32 us
    ppermute x1, starting transfers between devices, shards(): high = lax.ppermute(x_in, 'row', up)  3.09 us
  transfers between devices with their start and end apart: 13, of which 11 were waited for; matrix products, arithmetic and copies ran while one was open for 1% of the time, Pallas kernels for 4%

profile of v2, /device:TPU:2, one launch (start us, length us, event | category | flops | bytes accessed | tf_op | source)
XLA Modules:
  0.0 77.9 jit_solution(11941405682428959501)
XLA Ops:
  0.6 0.0 copy-start.5
  0.6 0.0 copy-start.6
  0.7 0.0 copy-start.7
  0.7 0.0 copy-start.8
  0.7 0.0 copy-start.4
  0.7 2.0 %pack.1 = bf16[16,64,256]{2,1,0:T(8,128)(2,1)} custom-call(bf16[2,2,8,16,16]{4,3,2,1,0:T(8,128)(2,1)} %lat_ref.1, bf16[2,2,8,16,256]{4,3,2,1,0:T(8,128)(2,1)} %mid_ref.1), custom_call_target="tpu_custom_call" | custom-call | tf_op jit(solution)/shard_map/pack/pallas_call | solution.py:279
  2.7 10.1 %all-to-all-start = ((bf16[16,64,256]{2,1,0:T(8,128)(2,1)}), bf16[16,64,256]{2,1,0:T(8,128)(2,1)S(1)}, u32[]{:S(2)}, u32[]{:S(2)}) async-start(bf16[16,64,256]{2,1,0:T(8,128)(2,1)} %pack.1), calls=%async_computation | async-start | bytes 1048576 | tf_op jit(solution)/shard_map/all_to_all | solution.py:283
  12.9 0.0 copy-start
  12.9 0.0 copy-done.5
  12.9 1.5 %collective-permute-start.1 = (bf16[3,144,256]{2,1,0:T(8,128)(2,1)S(1)}, bf16[3,144,256]{2,1,0:T(8,128)(2,1)S(1)}, u32[]{:S(2)}, u32[]{:S(2)}) collective-permute-start(bf16[3,144,256]{2,1,0:T(8,128)(2,1)S(1)} %bitcast.30), channel_id=1, source_target_pairs={{0,128},{128,0},{1,129},{129,1},{2,130},{130,2},{3,131},{131,3},{4... | collective-permute-start | bytes 663560 | tf_op jit(solution)/shard_map/ppermute | solution.py:285
  14.4 0.0 copy-done.6
  14.4 0.0 copy-done.7
  14.4 0.0 copy-done.8
  14.4 0.7 collective-permute-start.2
  15.1 0.0 copy-done.4
  15.1 0.3 copy.25.weight_ref
  15.5 0.0 copy-done
  15.5 0.6 head.1.part_ref
  16.1 0.0 copy-start.9
  16.1 0.0 copy-start.1
  16.1 0.0 copy-start.3
  16.1 1.5 %collective-permute-start = (f32[8,16,128]{2,1,0:T(8,128)S(1)}, f32[8,16,128]{2,1,0:T(8,128)S(1)}, u32[]{:S(2)}, u32[]{:S(2)}) collective-permute-start(f32[8,16,128]{2,1,0:T(8,128)S(1)} %head.1.part_ref), channel_id=1, source_target_pairs={{0,128},{128,0},{1,129},{129,1},{2,130},{130,2},{3,131},{131,3},{4... | collective-permute-start | bytes 196616 | tf_op jit(solution)/shard_map/ppermute | solution.py:302
  17.6 6.8 %collective-permute-done.2 = f32[3,256]{1,0:T(4,128)S(1)} collective-permute-done((f32[3,256]{1,0:T(4,128)S(1)}, f32[3,256]{1,0:T(4,128)S(1)}, u32[]{:S(2)}, u32[]{:S(2)}) %collective-permute-start.2) | collective-permute-done | bytes 3104 | tf_op jit(solution)/shard_map/ppermute | solution.py:285
  24.4 0.0 collective-permute-done.1
  24.4 0.1 maximum_select_fusion
  24.5 0.1 pad.4.weight_ref
  24.6 1.5 %collective-permute-done.rest_ref = f32[8,16,128]{2,1,0:T(8,128)S(1)} collective-permute-done((f32[8,16,128]{2,1,0:T(8,128)S(1)}, f32[8,16,128]{2,1,0:T(8,128)S(1)}, u32[]{:S(2)}, u32[]{:S(2)}) %collective-permute-start) | collective-permute-done | bytes 65568 | tf_op jit(solution)/shard_map/ppermute | solution.py:302
  26.1 4.0 %all-to-all-done.got_ref = bf16[16,64,256]{2,1,0:T(8,128)(2,1)S(1)} async-done(((bf16[16,64,256]{2,1,0:T(8,128)(2,1)}), bf16[16,64,256]{2,1,0:T(8,128)(2,1)S(1)}, u32[]{:S(2)}, u32[]{:S(2)}) %all-to-all-start) | async-done | bytes 524320 | tf_op jit(solution)/shard_map/all_to_all | solution.py:283
  30.1 0.0 collective-permute-start.3
  30.1 0.0 copy-done.9
  30.1 0.1 reshape.39
  30.1 0.1 broadcast_in_dim.7
  30.2 0.1 reshape.40.bias_ref
  30.3 0.1 pad_add_fusion.me_ref
  30.4 1.6 %collective-permute-done.3.twin_ref = bf16[16,64,256]{2,1,0:T(8,128)(2,1)S(1)} collective-permute-done((bf16[16,64,256]{2,1,0:T(8,128)(2,1)S(1)}, bf16[16,64,256]{2,1,0:T(8,128)(2,1)S(1)}, u32[]{:S(2)}, u32[]{:S(2)}) %collective-permute-start.3) | collective-permute-done | bytes 524320 | tf_op jit(solution)/shard_map/ppermute | solution.py:305
  32.0 0.0 copy-done.1
  32.0 0.0 copy-done.3
  32.0 1.8 %pick.1 = (bf16[32,32,256]{2,1,0:T(8,128)(2,1)}, bf16[2,6,16,128]{3,2,1,0:T(8,128)(2,1)S(1)}) custom-call(s32[3]{0:T(128)S(1)} %pad_add_fusion.me_ref, s32[64]{0:T(128)S(1)} %copy-done.3, s32[2]{0:T(128)S(1)} %copy-done.1, bf16[16,64,256]{2,1,0:T(8,128)(2,1)S(1)} %all-to-all-done.got_ref, bf16[16,64,256]{2,1,0:T(8,128)(2,1)S(1)} %collective-permute-done.3.twin_ref, ...), custom_call_target="tpu_custom_call" | custom-call | tf_op jit(solution)/shard_map/pick/pallas_call | solution.py:306
  33.8 0.0 copy-start.2
  33.8 7.4 %all-to-all-start.1 = ((bf16[32,32,256]{2,1,0:T(8,128)(2,1)}), bf16[32,32,256]{2,1,0:T(8,128)(2,1)S(1)}, u32[]{:S(2)}, u32[]{:S(2)}) async-start(bf16[32,32,256]{2,1,0:T(8,128)(2,1)} %get-tuple-element.27), calls=%async_computation.1 | async-start | bytes 1048576 | tf_op jit(solution)/shard_map/all_to_all | solution.py:319
  41.2 3.1 %collective-permute-start.5 = (bf16[2,6,16,128]{3,2,1,0:T(8,128)(2,1)S(1)}, bf16[2,6,16,128]{3,2,1,0:T(8,128)(2,1)S(1)}, u32[]{:S(2)}, u32[]{:S(2)}) collective-permute-start(bf16[2,6,16,128]{3,2,1,0:T(8,128)(2,1)S(1)} %get-tuple-element.22.x_ref), channel_id=1, source_target_pairs={{1,0},{2,1},{3,2},{0,3},{5,4},{6,5},{7,6},{4,7},{9,8},{10,9},{11,1... | collective-permute-start | bytes 147464 | tf_op jit(solution)/shard_map/ppermute | solution.py:322
  44.3 0.0 collective-permute-start.4
  44.3 1.7 %collective-permute-done.5.high_ref = bf16[2,6,16,128]{3,2,1,0:T(8,128)(2,1)S(1)} collective-permute-done((bf16[2,6,16,128]{3,2,1,0:T(8,128)(2,1)S(1)}, bf16[2,6,16,128]{3,2,1,0:T(8,128)(2,1)S(1)}, u32[]{:S(2)}, u32[]{:S(2)}) %collective-permute-start.5) | collective-permute-done | bytes 49184 | tf_op jit(solution)/shard_map/ppermute | solution.py:322
  46.0 3.5 %collective-permute-done.4.low_ref = bf16[2,6,16,128]{3,2,1,0:T(8,128)(2,1)S(1)} collective-permute-done((bf16[2,6,16,128]{3,2,1,0:T(8,128)(2,1)S(1)}, bf16[2,6,16,128]{3,2,1,0:T(8,128)(2,1)S(1)}, u32[]{:S(2)}, u32[]{:S(2)}) %collective-permute-start.4) | collective-permute-done | bytes 49184 | tf_op jit(solution)/shard_map/ppermute | solution.py:321
  49.6 2.9 %first.1 = (bf16[2,4,10,16,512]{4,3,2,1,0:T(8,128)(2,1)S(1)}, f32[4,512]{1,0:T(4,128)S(1)}, bf16[2,2,8,16,16]{4,3,2,1,0:T(8,128)(2,1)}) custom-call(s32[3]{0:T(128)S(1)} %pad_add_fusion.me_ref, bf16[2,6,16,128]{3,2,1,0:T(8,128)(2,1)S(1)} %get-tuple-element.22.x_ref, bf16[2,6,16,128]{3,2,1,0:T(8,128)(2,1)S(1)} %collective-permute-done.4.low_ref, ...), custom_call_target="tpu_custom_call" | custom-call | tf_op jit(solution)/shard_map/first/pallas_call | solution.py:323
  52.5 0.0 collective-permute-start.8
  52.5 0.9 %collective-permute-start.7 = (f32[4,512]{1,0:T(4,128)S(1)}, f32[4,512]{1,0:T(4,128)S(1)}, u32[]{:S(2)}, u32[]{:S(2)}) collective-permute-start(f32[4,512]{1,0:T(4,128)S(1)} %get-tuple-element.26.own_ref), channel_id=1, source_target_pairs={{0,2},{1,3},{2,0},{3,1},{4,6},{5,7},{6,4},{7,5},{8,10},{9,11},{10,... | collective-permute-start | bytes 24584 | tf_op jit(solution)/shard_map/ppermute | solution.py:336
  53.4 1.2 %collective-permute-start.6 = (f32[4,512]{1,0:T(4,128)S(1)}, f32[4,512]{1,0:T(4,128)S(1)}, u32[]{:S(2)}, u32[]{:S(2)}) collective-permute-start(f32[4,512]{1,0:T(4,128)S(1)} %get-tuple-element.26.own_ref), channel_id=1, source_target_pairs={{0,1},{1,2},{2,3},{3,0},{4,5},{5,6},{6,7},{7,4},{8,9},{9,10},{10,1... | collective-permute-start | bytes 24584 | tf_op jit(solution)/shard_map/ppermute | solution.py:336
  54.5 2.7 %all-to-all-done.1.pieces_ref = bf16[32,32,256]{2,1,0:T(8,128)(2,1)S(1)} async-done(((bf16[32,32,256]{2,1,0:T(8,128)(2,1)}), bf16[32,32,256]{2,1,0:T(8,128)(2,1)S(1)}, u32[]{:S(2)}, u32[]{:S(2)}) %all-to-all-start.1) | async-done | bytes 524320 | tf_op jit(solution)/shard_map/all_to_all | solution.py:319
  57.3 0.0 collective-permute-done.8.back_ref
  57.3 0.4 collective-permute-done.7.far_ref
  57.7 1.2 %collective-permute-done.6.near_ref = f32[4,512]{1,0:T(4,128)S(1)} collective-permute-done((f32[4,512]{1,0:T(4,128)S(1)}, f32[4,512]{1,0:T(4,128)S(1)}, u32[]{:S(2)}, u32[]{:S(2)}) %collective-permute-start.6) | collective-permute-done | bytes 8224 | tf_op jit(solution)/shard_map/ppermute | solution.py:336
  58.8 2.1 %collective-permute-start.10 = (bf16[2,2,32,256]{3,2,1,0:T(8,128)(2,1)S(1)}, bf16[2,2,32,256]{3,2,1,0:T(8,128)(2,1)S(1)}, u32[]{:S(2)}, u32[]{:S(2)}) collective-permute-start(bf16[2,2,32,256]{3,2,1,0:T(8,128)(2,1)S(1)} %get-tuple-element.33), channel_id=1, source_target_pairs={{1,0},{2,1},{3,2},{0,3},{5,4},{6,5},{7,6},{4,7},{9,8},{10,9},{11,1... | collective-permute-start | bytes 196616 | tf_op jit(solution)/shard_map/ppermute | solution.py:343
  60.9 0.0 collective-permute-start.9
  60.9 2.2 %collective-permute-done.10.high_ref = bf16[2,2,32,256]{3,2,1,0:T(8,128)(2,1)S(1)} collective-permute-done((bf16[2,2,32,256]{3,2,1,0:T(8,128)(2,1)S(1)}, bf16[2,2,32,256]{3,2,1,0:T(8,128)(2,1)S(1)}, u32[]{:S(2)}, u32[]{:S(2)}) %collective-permute-start.10) | collective-permute-done | bytes 65568 | tf_op jit(solution)/shard_map/ppermute | solution.py:343
  63.1 3.3 %collective-permute-done.9.low_ref = bf16[2,2,32,256]{3,2,1,0:T(8,128)(2,1)S(1)} collective-permute-done((bf16[2,2,32,256]{3,2,1,0:T(8,128)(2,1)S(1)}, bf16[2,2,32,256]{3,2,1,0:T(8,128)(2,1)S(1)}, u32[]{:S(2)}, u32[]{:S(2)}) %collective-permute-start.9) | collective-permute-done | bytes 65568 | tf_op jit(solution)/shard_map/ppermute | solution.py:341
  66.4 0.0 copy-done.2
  66.4 11.3 %block.1 = (bf16[2,4,8,16,256]{4,3,2,1,0:T(8,128)(2,1)}, bf16[2,2,8,16,256]{4,3,2,1,0:T(8,128)(2,1)}) custom-call(s32[3]{0:T(128)S(1)} %pad_add_fusion.me_ref, s32[2]{0:T(128)S(1)} %copy-done.1, bf16[2,4,10,16,512]{4,3,2,1,0:T(8,128)(2,1)S(1)} %get-tuple-element.25.first_ref, f32[4,512]{1,0:T(4,128)S(1)} %get-tuple-element.26.own_ref, ...), custom_call_target="tpu_custom_call" | custom-call | tf_op jit(solution)/shard_map/block/pallas_call | solution.py:346
  (8 shorter events, 0.1 us)
Async XLA Ops:
  0.6 12.2 %copy-start.5 = (bf16[3,3,3,16,256]{4,3,2,1,0:T(8,128)(2,1)S(1)}, bf16[3,3,3,16,256]{4,3,2,1,0:T(8,128)(2,1)}, u32[]{:S(2)}) copy-start(bf16[3,3,3,16,256]{4,3,2,1,0:T(8,128)(2,1)} %param.20) | copy-start | bytes 663556
  0.6 13.8 %copy-start.6 = (f32[256]{0:T(256)S(1)}, f32[256]{0:T(256)}, u32[]{:S(2)}) copy-start(f32[256]{0:T(256)} %param.23) | copy-start | bytes 3076
  0.7 13.8 %copy-start.7 = (f32[256]{0:T(256)S(1)}, f32[256]{0:T(256)}, u32[]{:S(2)}) copy-start(f32[256]{0:T(256)} %param.22) | copy-start | bytes 3076
  0.7 13.8 %copy-start.8 = (f32[256]{0:T(256)S(1)}, f32[256]{0:T(256)}, u32[]{:S(2)}) copy-start(f32[256]{0:T(256)} %param.21) | copy-start | bytes 3076
  0.7 14.4 %copy-start.4 = (bf16[2560,64]{0,1:T(8,128)(2,1)S(1)}, bf16[2560,64]{0,1:T(8,128)(2,1)}, u32[]{:S(2)}) copy-start(bf16[2560,64]{0,1:T(8,128)(2,1)} %param.14) | copy-start | bytes 983044
  2.7 27.3 %all-to-all-start = ((bf16[16,64,256]{2,1,0:T(8,128)(2,1)}), bf16[16,64,256]{2,1,0:T(8,128)(2,1)S(1)}, u32[]{:S(2)}, u32[]{:S(2)}) async-start(bf16[16,64,256]{2,1,0:T(8,128)(2,1)} %pack.1), calls=%async_computation | async-start | bytes 1048576 | tf_op jit(solution)/shard_map/all_to_all | solution.py:283
  12.9 2.6 %copy-start = (bf16[2,4,4,8,2560]{4,3,2,1,0:T(8,128)(2,1)S(1)}, bf16[2,4,4,8,2560]{4,3,2,1,0:T(8,128)(2,1)}, u32[]{:S(2)}) copy-start(bf16[2,4,4,8,2560]{4,3,2,1,0:T(8,128)(2,1)} %param.13) | copy-start | bytes 3932164
  12.9 11.5 %collective-permute-start.1 = (bf16[3,144,256]{2,1,0:T(8,128)(2,1)S(1)}, bf16[3,144,256]{2,1,0:T(8,128)(2,1)S(1)}, u32[]{:S(2)}, u32[]{:S(2)}) collective-permute-start(bf16[3,144,256]{2,1,0:T(8,128)(2,1)S(1)} %bitcast.30), channel_id=1, source_target_pairs={{0,128},{128,0},{1,129},{129,1},{2,130},{130,2},{3,131},{131,3},{4... | collective-permute-start | bytes 663560 | tf_op jit(solution)/shard_map/ppermute | solution.py:285
  14.4 9.9 %collective-permute-start.2 = (f32[3,256]{1,0:T(4,128)S(1)}, f32[3,256]{1,0:T(4,128)S(1)}, u32[]{:S(2)}, u32[]{:S(2)}) collective-permute-start(f32[3,256]{1,0:T(4,128)S(1)} %pad_maximum_fusion), channel_id=1, source_target_pairs={{0,128},{128,0},{1,129},{129,1},{2,130},{130,2},{3,131},{131,3},{4... | collective-permute-start | bytes 9224 | tf_op jit(solution)/shard_map/ppermute | solution.py:285
  16.1 14.0 %copy-start.9 = (f32[64]{0:T(128)S(1)}, f32[64]{0:T(128)}, u32[]{:S(2)}) copy-start(f32[64]{0:T(128)} %param.15) | copy-start | bytes 772
  16.1 15.9 %copy-start.1 = (s32[2]{0:T(128)S(1)}, s32[2]{0:T(128)}, u32[]{:S(2)}) copy-start(s32[2]{0:T(128)} %span_ref.3) | copy-start | bytes 28
  16.1 15.9 %copy-start.3 = (s32[64]{0:T(128)S(1)}, s32[64]{0:T(128)}, u32[]{:S(2)}) copy-start(s32[64]{0:T(128)} %moves_ref.1) | copy-start | bytes 772
  16.1 10.0 %collective-permute-start = (f32[8,16,128]{2,1,0:T(8,128)S(1)}, f32[8,16,128]{2,1,0:T(8,128)S(1)}, u32[]{:S(2)}, u32[]{:S(2)}) collective-permute-start(f32[8,16,128]{2,1,0:T(8,128)S(1)} %head.1.part_ref), channel_id=1, source_target_pairs={{0,128},{128,0},{1,129},{129,1},{2,130},{130,2},{3,131},{131,3},{4... | collective-permute-start | bytes 196616 | tf_op jit(solution)/shard_map/ppermute | solution.py:302
  30.1 1.9 %collective-permute-start.3 = (bf16[16,64,256]{2,1,0:T(8,128)(2,1)S(1)}, bf16[16,64,256]{2,1,0:T(8,128)(2,1)S(1)}, u32[]{:S(2)}, u32[]{:S(2)}) collective-permute-start(bf16[16,64,256]{2,1,0:T(8,128)(2,1)S(1)} %all-to-all-done.got_ref), channel_id=1, source_target_pairs={{0,4},{4,0},{8,12},{12,8},{16,20},{20,16},{24,28},{28,24},{32,36},... | collective-permute-start | bytes 1572872 | tf_op jit(solution)/shard_map/ppermute | solution.py:305
  33.8 32.6 %copy-start.2 = (f32[256]{0:T(256)S(1)}, f32[256]{0:T(256)}, u32[]{:S(2)}) copy-start(f32[256]{0:T(256)} %param.25) | copy-start | bytes 3076
  33.8 23.5 %all-to-all-start.1 = ((bf16[32,32,256]{2,1,0:T(8,128)(2,1)}), bf16[32,32,256]{2,1,0:T(8,128)(2,1)S(1)}, u32[]{:S(2)}, u32[]{:S(2)}) async-start(bf16[32,32,256]{2,1,0:T(8,128)(2,1)} %get-tuple-element.27), calls=%async_computation.1 | async-start | bytes 1048576 | tf_op jit(solution)/shard_map/all_to_all | solution.py:319
  41.2 4.8 %collective-permute-start.5 = (bf16[2,6,16,128]{3,2,1,0:T(8,128)(2,1)S(1)}, bf16[2,6,16,128]{3,2,1,0:T(8,128)(2,1)S(1)}, u32[]{:S(2)}, u32[]{:S(2)}) collective-permute-start(bf16[2,6,16,128]{3,2,1,0:T(8,128)(2,1)S(1)} %get-tuple-element.22.x_ref), channel_id=1, source_target_pairs={{1,0},{2,1},{3,2},{0,3},{5,4},{6,5},{7,6},{4,7},{9,8},{10,9},{11,1... | collective-permute-start | bytes 147464 | tf_op jit(solution)/shard_map/ppermute | solution.py:322
  44.3 5.3 %collective-permute-start.4 = (bf16[2,6,16,128]{3,2,1,0:T(8,128)(2,1)S(1)}, bf16[2,6,16,128]{3,2,1,0:T(8,128)(2,1)S(1)}, u32[]{:S(2)}, u32[]{:S(2)}) collective-permute-start(bf16[2,6,16,128]{3,2,1,0:T(8,128)(2,1)S(1)} %get-tuple-element.22.x_ref), channel_id=1, source_target_pairs={{0,1},{1,2},{2,3},{3,0},{4,5},{5,6},{6,7},{7,4},{8,9},{9,10},{10,1... | collective-permute-start | bytes 147464 | tf_op jit(solution)/shard_map/ppermute | solution.py:321
  52.5 4.8 %collective-permute-start.8 = (f32[4,512]{1,0:T(4,128)S(1)}, f32[4,512]{1,0:T(4,128)S(1)}, u32[]{:S(2)}, u32[]{:S(2)}) collective-permute-start(f32[4,512]{1,0:T(4,128)S(1)} %get-tuple-element.26.own_ref), channel_id=1, source_target_pairs={{0,3},{1,0},{2,1},{3,2},{4,7},{5,4},{6,5},{7,6},{8,11},{9,8},{10,9... | collective-permute-start | bytes 24584 | tf_op jit(solution)/shard_map/ppermute | solution.py:336
  52.5 5.2 %collective-permute-start.7 = (f32[4,512]{1,0:T(4,128)S(1)}, f32[4,512]{1,0:T(4,128)S(1)}, u32[]{:S(2)}, u32[]{:S(2)}) collective-permute-start(f32[4,512]{1,0:T(4,128)S(1)} %get-tuple-element.26.own_ref), channel_id=1, source_target_pairs={{0,2},{1,3},{2,0},{3,1},{4,6},{5,7},{6,4},{7,5},{8,10},{9,11},{10,... | collective-permute-start | bytes 24584 | tf_op jit(solution)/shard_map/ppermute | solution.py:336
  53.4 5.5 %collective-permute-start.6 = (f32[4,512]{1,0:T(4,128)S(1)}, f32[4,512]{1,0:T(4,128)S(1)}, u32[]{:S(2)}, u32[]{:S(2)}) collective-permute-start(f32[4,512]{1,0:T(4,128)S(1)} %get-tuple-element.26.own_ref), channel_id=1, source_target_pairs={{0,1},{1,2},{2,3},{3,0},{4,5},{5,6},{6,7},{7,4},{8,9},{9,10},{10,1... | collective-permute-start | bytes 24584 | tf_op jit(solution)/shard_map/ppermute | solution.py:336
  58.8 4.3 %collective-permute-start.10 = (bf16[2,2,32,256]{3,2,1,0:T(8,128)(2,1)S(1)}, bf16[2,2,32,256]{3,2,1,0:T(8,128)(2,1)S(1)}, u32[]{:S(2)}, u32[]{:S(2)}) collective-permute-start(bf16[2,2,32,256]{3,2,1,0:T(8,128)(2,1)S(1)} %get-tuple-element.33), channel_id=1, source_target_pairs={{1,0},{2,1},{3,2},{0,3},{5,4},{6,5},{7,6},{4,7},{9,8},{10,9},{11,1... | collective-permute-start | bytes 196616 | tf_op jit(solution)/shard_map/ppermute | solution.py:343
  60.9 5.5 %collective-permute-start.9 = (bf16[2,2,32,256]{3,2,1,0:T(8,128)(2,1)S(1)}, bf16[2,2,32,256]{3,2,1,0:T(8,128)(2,1)S(1)}, u32[]{:S(2)}, u32[]{:S(2)}) collective-permute-start(bf16[2,2,32,256]{3,2,1,0:T(8,128)(2,1)S(1)} %get-tuple-element.37), channel_id=1, source_target_pairs={{0,1},{1,2},{2,3},{3,0},{4,5},{5,6},{6,7},{7,4},{8,9},{9,10},{10,1... | collective-permute-start | bytes 196616 | tf_op jit(solution)/shard_map/ppermute | solution.py:341

commit v3 on v2

--- a/solution.py
+++ b/solution.py
@@ -43,17 +43,27 @@
             out_ref[frame, pl.ds(q, 8, stride=2), :] = jnp.concatenate(parts, axis=1)
 
 
-def pack_kernel(lat_ref, mid_ref, out_ref):
-    both = []
+def pack_kernel(lat_ref, mid_ref, out_ref, lat, spread, moved, sems):
+    fetched = [pltpu.make_async_copy(lat_ref, lat, sems.at[0])] + [
+        pltpu.make_async_copy(mid_ref.at[k], moved.at[:, pl.ds(k * 16, 16), :], sems.at[1 + k])
+        for k in range(2)
+    ]
+    for copy in fetched:
+        copy.start()
+    fetched[0].wait()
     for frame in range(2):
-        rows = [lat_ref[k, frame, r] for k in range(2) for r in range(8)]
-        both.append(jnp.concatenate(rows, axis=1))
-    for piece in range(16):
-        frame, row = divmod(piece, 8)
-        for k in range(2):
-            out_ref[piece, k * 16 : (k + 1) * 16, :] = mid_ref[k, frame, row]
-        for frame in range(2):
-            out_ref[piece, 32 + frame * 16 : 48 + frame * 16, :] = both[frame]
+        rows = [lat[k, frame, r] for k in range(2) for r in range(8)]
+        both = jnp.concatenate(rows, axis=1)
+        for piece in range(16):
+            spread[piece, frame * 16 : (frame + 1) * 16, :] = both
+    last = [pltpu.make_async_copy(spread, out_ref.at[:, pl.ds(32, 32), :], sems.at[3])]
+    last[0].start()
+    fetched[1].wait()
+    fetched[2].wait()
+    last.append(pltpu.make_async_copy(moved, out_ref.at[:, pl.ds(0, 32), :], sems.at[4]))
+    last[1].start()
+    for copy in last:
+        copy.wait()
 
 
 def pick_kernel(
@@ -277,8 +287,19 @@
     me = jnp.stack([dec, section, row]).astype(jnp.int32)
 
     send = call(
-        pack_kernel, "pack", shape((hosts, 64, part), BF16), [VMEM, VMEM], limit=60
-    )(lat_cache, mid_cache)
+        pack_kernel,
+        "pack",
+        shape((hosts, 64, part), BF16),
+        [ANY, ANY],
+        ANY,
+        [
+            pltpu.VMEM(lat_cache.shape, BF16),
+            pltpu.VMEM((hosts, 32, part), BF16),
+            pltpu.VMEM((hosts, 32, part), BF16),
+            pltpu.SemaphoreType.DMA((5,)),
+        ],
+        limit=60,
+    )(lat_cache, mid_cache.reshape(streams, hosts, cols, part))
     spread = [[2 * j + c for j in range(hosts)] for c in range(2)]
     got = lax.all_to_all(send, "dec", 0, 0, axis_index_groups=spread)
     def whole(own):

time: 79.3 us -> 79.3 us (level)
  no operation moved by 1% of the time
where the time goes in v3:
time: 79.3 us; the launch traced here: 77.8 us
  waiting for transfers between devices  28.8 us (36%)
  starting transfers between devices  28.5 us (36%)
  Pallas kernels  18.6 us (23%)
  between operations  0.98 us (1%)
    pallas_call x1, Pallas kernels, shards(): call(functools.partial(block_kernel, count), 'block', (shape((streams, fr...  11.3 us
    all_to_all x1, starting transfers between devices, shards(): got = lax.all_to_all(send, 'dec', 0, 0, axis_index_groups=spread)  10.1 us
    all_to_all x1, starting transfers between devices, shards(): lax.all_to_all(back, ('section', 'dec'), 0, 0, axis_index_groups=gather)  7.43 us
    ppermute x2, waiting for transfers between devices, whole(): other = lax.ppermute(own, 'section', SWAP)  6.76 us
    all_to_all x1, waiting for transfers between devices, shards(): got = lax.all_to_all(send, 'dec', 0, 0, axis_index_groups=spread)  4 us
    ppermute x1, waiting for transfers between devices, shards(): low = lax.ppermute(x_in, 'row', down)  3.55 us
    ppermute x1, waiting for transfers between devices, shards(): low_mid = lax.ppermute(edges[:, :, rows - 1], 'row', down)  3.32 us
    ppermute x1, starting transfers between devices, shards(): high = lax.ppermute(x_in, 'row', up)  3.09 us
  transfers between devices with their start and end apart: 13, of which 11 were waited for; matrix products, arithmetic and copies ran while one was open for 1% of the time, Pallas kernels for 4%

profile of v3, /device:TPU:2, one launch (start us, length us, event | category | flops | bytes accessed | tf_op | source)
XLA Modules:
  0.0 77.8 jit_solution(8943329449301025295)
XLA Ops:
  0.6 0.0 copy-start.5
  0.6 0.0 copy-start.6
  0.7 0.0 copy-start.7
  0.7 0.0 copy-start.8
  0.7 0.0 copy-start.4
  0.7 2.0 %pack.1 = bf16[16,64,256]{2,1,0:T(8,128)(2,1)} custom-call(bf16[2,2,8,16,16]{4,3,2,1,0:T(8,128)(2,1)} %lat_ref.1, bf16[2,16,16,256]{3,2,1,0:T(8,128)(2,1)} %bitcast.34), custom_call_target="tpu_custom_call" | custom-call | tf_op jit(solution)/shard_map/pack/pallas_call | solution.py:289
  2.6 10.1 %all-to-all-start = ((bf16[16,64,256]{2,1,0:T(8,128)(2,1)}), bf16[16,64,256]{2,1,0:T(8,128)(2,1)S(1)}, u32[]{:S(2)}, u32[]{:S(2)}) async-start(bf16[16,64,256]{2,1,0:T(8,128)(2,1)} %pack.1), calls=%async_computation | async-start | bytes 1048576 | tf_op jit(solution)/shard_map/all_to_all | solution.py:304
  12.8 0.0 copy-start
  12.8 0.0 copy-done.5
  12.8 1.5 %collective-permute-start.1 = (bf16[3,144,256]{2,1,0:T(8,128)(2,1)S(1)}, bf16[3,144,256]{2,1,0:T(8,128)(2,1)S(1)}, u32[]{:S(2)}, u32[]{:S(2)}) collective-permute-start(bf16[3,144,256]{2,1,0:T(8,128)(2,1)S(1)} %bitcast.31), channel_id=1, source_target_pairs={{0,128},{128,0},{1,129},{129,1},{2,130},{130,2},{3,131},{131,3},{4... | collective-permute-start | bytes 663560 | tf_op jit(solution)/shard_map/ppermute | solution.py:306
  14.4 0.0 copy-done.6
  14.4 0.0 copy-done.7
  14.4 0.0 copy-done.8
  14.4 0.7 collective-permute-start.2
  15.1 0.0 copy-done.4
  15.1 0.3 copy.25.weight_ref
  15.4 0.0 copy-done
  15.4 0.6 head.1.part_ref
  16.0 0.0 copy-start.9
  16.0 0.0 copy-start.1
  16.0 0.0 copy-start.3
  16.0 1.5 %collective-permute-start = (f32[8,16,128]{2,1,0:T(8,128)S(1)}, f32[8,16,128]{2,1,0:T(8,128)S(1)}, u32[]{:S(2)}, u32[]{:S(2)}) collective-permute-start(f32[8,16,128]{2,1,0:T(8,128)S(1)} %head.1.part_ref), channel_id=1, source_target_pairs={{0,128},{128,0},{1,129},{129,1},{2,130},{130,2},{3,131},{131,3},{4... | collective-permute-start | bytes 196616 | tf_op jit(solution)/shard_map/ppermute | solution.py:323
  17.6 6.8 %collective-permute-done.2 = f32[3,256]{1,0:T(4,128)S(1)} collective-permute-done((f32[3,256]{1,0:T(4,128)S(1)}, f32[3,256]{1,0:T(4,128)S(1)}, u32[]{:S(2)}, u32[]{:S(2)}) %collective-permute-start.2) | collective-permute-done | bytes 3104 | tf_op jit(solution)/shard_map/ppermute | solution.py:306
  24.3 0.0 collective-permute-done.1
  24.3 0.1 maximum_select_fusion
  24.5 0.1 pad.4.weight_ref
  24.5 1.5 %collective-permute-done.rest_ref = f32[8,16,128]{2,1,0:T(8,128)S(1)} collective-permute-done((f32[8,16,128]{2,1,0:T(8,128)S(1)}, f32[8,16,128]{2,1,0:T(8,128)S(1)}, u32[]{:S(2)}, u32[]{:S(2)}) %collective-permute-start) | collective-permute-done | bytes 65568 | tf_op jit(solution)/shard_map/ppermute | solution.py:323
  26.0 4.0 %all-to-all-done.got_ref = bf16[16,64,256]{2,1,0:T(8,128)(2,1)S(1)} async-done(((bf16[16,64,256]{2,1,0:T(8,128)(2,1)}), bf16[16,64,256]{2,1,0:T(8,128)(2,1)S(1)}, u32[]{:S(2)}, u32[]{:S(2)}) %all-to-all-start) | async-done | bytes 524320 | tf_op jit(solution)/shard_map/all_to_all | solution.py:304
  30.0 0.0 collective-permute-start.3
  30.0 0.0 copy-done.9
  30.0 0.1 reshape.43
  30.1 0.1 broadcast_in_dim.7
  30.2 0.1 reshape.44.bias_ref
  30.3 0.1 pad_add_fusion.me_ref
  30.3 1.6 %collective-permute-done.3.twin_ref = bf16[16,64,256]{2,1,0:T(8,128)(2,1)S(1)} collective-permute-done((bf16[16,64,256]{2,1,0:T(8,128)(2,1)S(1)}, bf16[16,64,256]{2,1,0:T(8,128)(2,1)S(1)}, u32[]{:S(2)}, u32[]{:S(2)}) %collective-permute-start.3) | collective-permute-done | bytes 524320 | tf_op jit(solution)/shard_map/ppermute | solution.py:326
  31.9 0.0 copy-done.1
  31.9 0.0 copy-done.3
  31.9 1.8 %pick.1 = (bf16[32,32,256]{2,1,0:T(8,128)(2,1)}, bf16[2,6,16,128]{3,2,1,0:T(8,128)(2,1)S(1)}) custom-call(s32[3]{0:T(128)S(1)} %pad_add_fusion.me_ref, s32[64]{0:T(128)S(1)} %copy-done.3, s32[2]{0:T(128)S(1)} %copy-done.1, bf16[16,64,256]{2,1,0:T(8,128)(2,1)S(1)} %all-to-all-done.got_ref, bf16[16,64,256]{2,1,0:T(8,128)(2,1)S(1)} %collective-permute-done.3.twin_ref, ...), custom_call_target="tpu_custom_call" | custom-call | tf_op jit(solution)/shard_map/pick/pallas_call | solution.py:327
  33.7 0.0 copy-start.2
  33.7 7.4 %all-to-all-start.1 = ((bf16[32,32,256]{2,1,0:T(8,128)(2,1)}), bf16[32,32,256]{2,1,0:T(8,128)(2,1)S(1)}, u32[]{:S(2)}, u32[]{:S(2)}) async-start(bf16[32,32,256]{2,1,0:T(8,128)(2,1)} %get-tuple-element.27), calls=%async_computation.1 | async-start | bytes 1048576 | tf_op jit(solution)/shard_map/all_to_all | solution.py:340
  41.2 3.1 %collective-permute-start.5 = (bf16[2,6,16,128]{3,2,1,0:T(8,128)(2,1)S(1)}, bf16[2,6,16,128]{3,2,1,0:T(8,128)(2,1)S(1)}, u32[]{:S(2)}, u32[]{:S(2)}) collective-permute-start(bf16[2,6,16,128]{3,2,1,0:T(8,128)(2,1)S(1)} %get-tuple-element.22.x_ref), channel_id=1, source_target_pairs={{1,0},{2,1},{3,2},{0,3},{5,4},{6,5},{7,6},{4,7},{9,8},{10,9},{11,1... | collective-permute-start | bytes 147464 | tf_op jit(solution)/shard_map/ppermute | solution.py:343
  44.2 0.0 collective-permute-start.4
  44.3 1.7 %collective-permute-done.5.high_ref = bf16[2,6,16,128]{3,2,1,0:T(8,128)(2,1)S(1)} collective-permute-done((bf16[2,6,16,128]{3,2,1,0:T(8,128)(2,1)S(1)}, bf16[2,6,16,128]{3,2,1,0:T(8,128)(2,1)S(1)}, u32[]{:S(2)}, u32[]{:S(2)}) %collective-permute-start.5) | collective-permute-done | bytes 49184 | tf_op jit(solution)/shard_map/ppermute | solution.py:343
  46.0 3.5 %collective-permute-done.4.low_ref = bf16[2,6,16,128]{3,2,1,0:T(8,128)(2,1)S(1)} collective-permute-done((bf16[2,6,16,128]{3,2,1,0:T(8,128)(2,1)S(1)}, bf16[2,6,16,128]{3,2,1,0:T(8,128)(2,1)S(1)}, u32[]{:S(2)}, u32[]{:S(2)}) %collective-permute-start.4) | collective-permute-done | bytes 49184 | tf_op jit(solution)/shard_map/ppermute | solution.py:342
  49.5 2.9 %first.1 = (bf16[2,4,10,16,512]{4,3,2,1,0:T(8,128)(2,1)S(1)}, f32[4,512]{1,0:T(4,128)S(1)}, bf16[2,2,8,16,16]{4,3,2,1,0:T(8,128)(2,1)}) custom-call(s32[3]{0:T(128)S(1)} %pad_add_fusion.me_ref, bf16[2,6,16,128]{3,2,1,0:T(8,128)(2,1)S(1)} %get-tuple-element.22.x_ref, bf16[2,6,16,128]{3,2,1,0:T(8,128)(2,1)S(1)} %collective-permute-done.4.low_ref, ...), custom_call_target="tpu_custom_call" | custom-call | tf_op jit(solution)/shard_map/first/pallas_call | solution.py:344
  52.5 0.0 collective-permute-start.8
  52.5 0.9 %collective-permute-start.7 = (f32[4,512]{1,0:T(4,128)S(1)}, f32[4,512]{1,0:T(4,128)S(1)}, u32[]{:S(2)}, u32[]{:S(2)}) collective-permute-start(f32[4,512]{1,0:T(4,128)S(1)} %get-tuple-element.26.own_ref), channel_id=1, source_target_pairs={{0,2},{1,3},{2,0},{3,1},{4,6},{5,7},{6,4},{7,5},{8,10},{9,11},{10,... | collective-permute-start | bytes 24584 | tf_op jit(solution)/shard_map/ppermute | solution.py:357
  53.3 1.2 %collective-permute-start.6 = (f32[4,512]{1,0:T(4,128)S(1)}, f32[4,512]{1,0:T(4,128)S(1)}, u32[]{:S(2)}, u32[]{:S(2)}) collective-permute-start(f32[4,512]{1,0:T(4,128)S(1)} %get-tuple-element.26.own_ref), channel_id=1, source_target_pairs={{0,1},{1,2},{2,3},{3,0},{4,5},{5,6},{6,7},{7,4},{8,9},{9,10},{10,1... | collective-permute-start | bytes 24584 | tf_op jit(solution)/shard_map/ppermute | solution.py:357
  54.5 2.7 %all-to-all-done.1.pieces_ref = bf16[32,32,256]{2,1,0:T(8,128)(2,1)S(1)} async-done(((bf16[32,32,256]{2,1,0:T(8,128)(2,1)}), bf16[32,32,256]{2,1,0:T(8,128)(2,1)S(1)}, u32[]{:S(2)}, u32[]{:S(2)}) %all-to-all-start.1) | async-done | bytes 524320 | tf_op jit(solution)/shard_map/all_to_all | solution.py:340
  57.2 0.0 collective-permute-done.8.back_ref
  57.2 0.4 collective-permute-done.7.far_ref
  57.6 1.2 %collective-permute-done.6.near_ref = f32[4,512]{1,0:T(4,128)S(1)} collective-permute-done((f32[4,512]{1,0:T(4,128)S(1)}, f32[4,512]{1,0:T(4,128)S(1)}, u32[]{:S(2)}, u32[]{:S(2)}) %collective-permute-start.6) | collective-permute-done | bytes 8224 | tf_op jit(solution)/shard_map/ppermute | solution.py:357
  58.8 2.1 %collective-permute-start.10 = (bf16[2,2,32,256]{3,2,1,0:T(8,128)(2,1)S(1)}, bf16[2,2,32,256]{3,2,1,0:T(8,128)(2,1)S(1)}, u32[]{:S(2)}, u32[]{:S(2)}) collective-permute-start(bf16[2,2,32,256]{3,2,1,0:T(8,128)(2,1)S(1)} %get-tuple-element.33), channel_id=1, source_target_pairs={{1,0},{2,1},{3,2},{0,3},{5,4},{6,5},{7,6},{4,7},{9,8},{10,9},{11,1... | collective-permute-start | bytes 196616 | tf_op jit(solution)/shard_map/ppermute | solution.py:364
  60.9 0.0 collective-permute-start.9
  60.9 2.2 %collective-permute-done.10.high_ref = bf16[2,2,32,256]{3,2,1,0:T(8,128)(2,1)S(1)} collective-permute-done((bf16[2,2,32,256]{3,2,1,0:T(8,128)(2,1)S(1)}, bf16[2,2,32,256]{3,2,1,0:T(8,128)(2,1)S(1)}, u32[]{:S(2)}, u32[]{:S(2)}) %collective-permute-start.10) | collective-permute-done | bytes 65568 | tf_op jit(solution)/shard_map/ppermute | solution.py:364
  63.0 3.3 %collective-permute-done.9.low_ref = bf16[2,2,32,256]{3,2,1,0:T(8,128)(2,1)S(1)} collective-permute-done((bf16[2,2,32,256]{3,2,1,0:T(8,128)(2,1)S(1)}, bf16[2,2,32,256]{3,2,1,0:T(8,128)(2,1)S(1)}, u32[]{:S(2)}, u32[]{:S(2)}) %collective-permute-start.9) | collective-permute-done | bytes 65568 | tf_op jit(solution)/shard_map/ppermute | solution.py:362
  66.4 0.0 copy-done.2
  66.4 11.3 %block.1 = (bf16[2,4,8,16,256]{4,3,2,1,0:T(8,128)(2,1)}, bf16[2,2,8,16,256]{4,3,2,1,0:T(8,128)(2,1)}) custom-call(s32[3]{0:T(128)S(1)} %pad_add_fusion.me_ref, s32[2]{0:T(128)S(1)} %copy-done.1, bf16[2,4,10,16,512]{4,3,2,1,0:T(8,128)(2,1)S(1)} %get-tuple-element.25.first_ref, f32[4,512]{1,0:T(4,128)S(1)} %get-tuple-element.26.own_ref, ...), custom_call_target="tpu_custom_call" | custom-call | tf_op jit(solution)/shard_map/block/pallas_call | solution.py:367
  (8 shorter events, 0.1 us)
Async XLA Ops:
  0.6 12.2 %copy-start.5 = (bf16[3,3,3,16,256]{4,3,2,1,0:T(8,128)(2,1)S(1)}, bf16[3,3,3,16,256]{4,3,2,1,0:T(8,128)(2,1)}, u32[]{:S(2)}) copy-start(bf16[3,3,3,16,256]{4,3,2,1,0:T(8,128)(2,1)} %param.20) | copy-start | bytes 663556
  0.6 13.7 %copy-start.6 = (f32[256]{0:T(256)S(1)}, f32[256]{0:T(256)}, u32[]{:S(2)}) copy-start(f32[256]{0:T(256)} %param.23) | copy-start | bytes 3076
  0.7 13.7 %copy-start.7 = (f32[256]{0:T(256)S(1)}, f32[256]{0:T(256)}, u32[]{:S(2)}) copy-start(f32[256]{0:T(256)} %param.22) | copy-start | bytes 3076
  0.7 13.7 %copy-start.8 = (f32[256]{0:T(256)S(1)}, f32[256]{0:T(256)}, u32[]{:S(2)}) copy-start(f32[256]{0:T(256)} %param.21) | copy-start | bytes 3076
  0.7 14.4 %copy-start.4 = (bf16[2560,64]{0,1:T(8,128)(2,1)S(1)}, bf16[2560,64]{0,1:T(8,128)(2,1)}, u32[]{:S(2)}) copy-start(bf16[2560,64]{0,1:T(8,128)(2,1)} %param.14) | copy-start | bytes 983044
  2.6 27.3 %all-to-all-start = ((bf16[16,64,256]{2,1,0:T(8,128)(2,1)}), bf16[16,64,256]{2,1,0:T(8,128)(2,1)S(1)}, u32[]{:S(2)}, u32[]{:S(2)}) async-start(bf16[16,64,256]{2,1,0:T(8,128)(2,1)} %pack.1), calls=%async_computation | async-start | bytes 1048576 | tf_op jit(solution)/shard_map/all_to_all | solution.py:304
  12.8 2.6 %copy-start = (bf16[2,4,4,8,2560]{4,3,2,1,0:T(8,128)(2,1)S(1)}, bf16[2,4,4,8,2560]{4,3,2,1,0:T(8,128)(2,1)}, u32[]{:S(2)}) copy-start(bf16[2,4,4,8,2560]{4,3,2,1,0:T(8,128)(2,1)} %param.13) | copy-start | bytes 3932164
  12.8 11.5 %collective-permute-start.1 = (bf16[3,144,256]{2,1,0:T(8,128)(2,1)S(1)}, bf16[3,144,256]{2,1,0:T(8,128)(2,1)S(1)}, u32[]{:S(2)}, u32[]{:S(2)}) collective-permute-start(bf16[3,144,256]{2,1,0:T(8,128)(2,1)S(1)} %bitcast.31), channel_id=1, source_target_pairs={{0,128},{128,0},{1,129},{129,1},{2,130},{130,2},{3,131},{131,3},{4... | collective-permute-start | bytes 663560 | tf_op jit(solution)/shard_map/ppermute | solution.py:306
  14.4 9.9 %collective-permute-start.2 = (f32[3,256]{1,0:T(4,128)S(1)}, f32[3,256]{1,0:T(4,128)S(1)}, u32[]{:S(2)}, u32[]{:S(2)}) collective-permute-start(f32[3,256]{1,0:T(4,128)S(1)} %pad_maximum_fusion), channel_id=1, source_target_pairs={{0,128},{128,0},{1,129},{129,1},{2,130},{130,2},{3,131},{131,3},{4... | collective-permute-start | bytes 9224 | tf_op jit(solution)/shard_map/ppermute | solution.py:306
  16.0 14.0 %copy-start.9 = (f32[64]{0:T(128)S(1)}, f32[64]{0:T(128)}, u32[]{:S(2)}) copy-start(f32[64]{0:T(128)} %param.15) | copy-start | bytes 772
  16.0 15.9 %copy-start.1 = (s32[2]{0:T(128)S(1)}, s32[2]{0:T(128)}, u32[]{:S(2)}) copy-start(s32[2]{0:T(128)} %span_ref.3) | copy-start | bytes 28
  16.0 15.9 %copy-start.3 = (s32[64]{0:T(128)S(1)}, s32[64]{0:T(128)}, u32[]{:S(2)}) copy-start(s32[64]{0:T(128)} %moves_ref.1) | copy-start | bytes 772
  16.0 10.0 %collective-permute-start = (f32[8,16,128]{2,1,0:T(8,128)S(1)}, f32[8,16,128]{2,1,0:T(8,128)S(1)}, u32[]{:S(2)}, u32[]{:S(2)}) collective-permute-start(f32[8,16,128]{2,1,0:T(8,128)S(1)} %head.1.part_ref), channel_id=1, source_target_pairs={{0,128},{128,0},{1,129},{129,1},{2,130},{130,2},{3,131},{131,3},{4... | collective-permute-start | bytes 196616 | tf_op jit(solution)/shard_map/ppermute | solution.py:323
  30.0 1.9 %collective-permute-start.3 = (bf16[16,64,256]{2,1,0:T(8,128)(2,1)S(1)}, bf16[16,64,256]{2,1,0:T(8,128)(2,1)S(1)}, u32[]{:S(2)}, u32[]{:S(2)}) collective-permute-start(bf16[16,64,256]{2,1,0:T(8,128)(2,1)S(1)} %all-to-all-done.got_ref), channel_id=1, source_target_pairs={{0,4},{4,0},{8,12},{12,8},{16,20},{20,16},{24,28},{28,24},{32,36},... | collective-permute-start | bytes 1572872 | tf_op jit(solution)/shard_map/ppermute | solution.py:326
  33.7 32.6 %copy-start.2 = (f32[256]{0:T(256)S(1)}, f32[256]{0:T(256)}, u32[]{:S(2)}) copy-start(f32[256]{0:T(256)} %param.25) | copy-start | bytes 3076
  33.7 23.5 %all-to-all-start.1 = ((bf16[32,32,256]{2,1,0:T(8,128)(2,1)}), bf16[32,32,256]{2,1,0:T(8,128)(2,1)S(1)}, u32[]{:S(2)}, u32[]{:S(2)}) async-start(bf16[32,32,256]{2,1,0:T(8,128)(2,1)} %get-tuple-element.27), calls=%async_computation.1 | async-start | bytes 1048576 | tf_op jit(solution)/shard_map/all_to_all | solution.py:340
  41.2 4.8 %collective-permute-start.5 = (bf16[2,6,16,128]{3,2,1,0:T(8,128)(2,1)S(1)}, bf16[2,6,16,128]{3,2,1,0:T(8,128)(2,1)S(1)}, u32[]{:S(2)}, u32[]{:S(2)}) collective-permute-start(bf16[2,6,16,128]{3,2,1,0:T(8,128)(2,1)S(1)} %get-tuple-element.22.x_ref), channel_id=1, source_target_pairs={{1,0},{2,1},{3,2},{0,3},{5,4},{6,5},{7,6},{4,7},{9,8},{10,9},{11,1... | collective-permute-start | bytes 147464 | tf_op jit(solution)/shard_map/ppermute | solution.py:343
  44.2 5.3 %collective-permute-start.4 = (bf16[2,6,16,128]{3,2,1,0:T(8,128)(2,1)S(1)}, bf16[2,6,16,128]{3,2,1,0:T(8,128)(2,1)S(1)}, u32[]{:S(2)}, u32[]{:S(2)}) collective-permute-start(bf16[2,6,16,128]{3,2,1,0:T(8,128)(2,1)S(1)} %get-tuple-element.22.x_ref), channel_id=1, source_target_pairs={{0,1},{1,2},{2,3},{3,0},{4,5},{5,6},{6,7},{7,4},{8,9},{9,10},{10,1... | collective-permute-start | bytes 147464 | tf_op jit(solution)/shard_map/ppermute | solution.py:342
  52.5 4.8 %collective-permute-start.8 = (f32[4,512]{1,0:T(4,128)S(1)}, f32[4,512]{1,0:T(4,128)S(1)}, u32[]{:S(2)}, u32[]{:S(2)}) collective-permute-start(f32[4,512]{1,0:T(4,128)S(1)} %get-tuple-element.26.own_ref), channel_id=1, source_target_pairs={{0,3},{1,0},{2,1},{3,2},{4,7},{5,4},{6,5},{7,6},{8,11},{9,8},{10,9... | collective-permute-start | bytes 24584 | tf_op jit(solution)/shard_map/ppermute | solution.py:357
  52.5 5.2 %collective-permute-start.7 = (f32[4,512]{1,0:T(4,128)S(1)}, f32[4,512]{1,0:T(4,128)S(1)}, u32[]{:S(2)}, u32[]{:S(2)}) collective-permute-start(f32[4,512]{1,0:T(4,128)S(1)} %get-tuple-element.26.own_ref), channel_id=1, source_target_pairs={{0,2},{1,3},{2,0},{3,1},{4,6},{5,7},{6,4},{7,5},{8,10},{9,11},{10,... | collective-permute-start | bytes 24584 | tf_op jit(solution)/shard_map/ppermute | solution.py:357
  53.3 5.5 %collective-permute-start.6 = (f32[4,512]{1,0:T(4,128)S(1)}, f32[4,512]{1,0:T(4,128)S(1)}, u32[]{:S(2)}, u32[]{:S(2)}) collective-permute-start(f32[4,512]{1,0:T(4,128)S(1)} %get-tuple-element.26.own_ref), channel_id=1, source_target_pairs={{0,1},{1,2},{2,3},{3,0},{4,5},{5,6},{6,7},{7,4},{8,9},{9,10},{10,1... | collective-permute-start | bytes 24584 | tf_op jit(solution)/shard_map/ppermute | solution.py:357
  58.8 4.3 %collective-permute-start.10 = (bf16[2,2,32,256]{3,2,1,0:T(8,128)(2,1)S(1)}, bf16[2,2,32,256]{3,2,1,0:T(8,128)(2,1)S(1)}, u32[]{:S(2)}, u32[]{:S(2)}) collective-permute-start(bf16[2,2,32,256]{3,2,1,0:T(8,128)(2,1)S(1)} %get-tuple-element.33), channel_id=1, source_target_pairs={{1,0},{2,1},{3,2},{0,3},{5,4},{6,5},{7,6},{4,7},{9,8},{10,9},{11,1... | collective-permute-start | bytes 196616 | tf_op jit(solution)/shard_map/ppermute | solution.py:364
  60.9 5.5 %collective-permute-start.9 = (bf16[2,2,32,256]{3,2,1,0:T(8,128)(2,1)S(1)}, bf16[2,2,32,256]{3,2,1,0:T(8,128)(2,1)S(1)}, u32[]{:S(2)}, u32[]{:S(2)}) collective-permute-start(bf16[2,2,32,256]{3,2,1,0:T(8,128)(2,1)S(1)} %get-tuple-element.37), channel_id=1, source_target_pairs={{0,1},{1,2},{2,3},{3,0},{4,5},{5,6},{6,7},{7,4},{8,9},{9,10},{10,1... | collective-permute-start | bytes 196616 | tf_op jit(solution)/shard_map/ppermute | solution.py:362

commit v4 on v2

--- a/solution.py
+++ b/solution.py
@@ -244,7 +244,7 @@
 
 def beside():
     count = lax.axis_size("row")
-    down = [(i, (i + 1) % count) for i in range(count)]
+    down = [(i, i + 1) for i in range(count - 1)]
     up = [((i + 1) % count, i) for i in range(count)]
     return down, up
 

time: 79.3 us -> 77.9 us (0.982)
  waiting for transfers between devices: 28.8 us -> 21.5 us
  starting transfers between devices: 28.5 us -> 34.8 us
    ppermute x1, starting transfers between devices: 0.01 us -> 3.21 us  [shards(): low_mid = lax.ppermute(edges[:, :, rows - 1], 'row', down)]
    ppermute x3, starting transfers between devices: 2.03 us -> 5.01 us  [shards(): lax.ppermute(stats, 'row', [(i, (i + shift) % bands) for i in range(bands)])]
    ppermute x1, waiting for transfers between devices: 3.55 us -> 1.27 us  [shards(): low = lax.ppermute(x_in, 'row', down)]
    ppermute x1, waiting for transfers between devices: 2.15 us -> 0.16 us  [shards(): high_mid = lax.ppermute(edge, 'row', up)]
    ppermute x1, waiting for transfers between devices: 3.32 us -> 1.55 us  [shards(): low_mid = lax.ppermute(edges[:, :, rows - 1], 'row', down)]
    ppermute x1, waiting for transfers between devices: 1.75 us -> 0.45 us  [shards(): high = lax.ppermute(x_in, 'row', up)]
    ppermute x1, starting transfers between devices: 0.01 us -> 1.28 us  [shards(): low = lax.ppermute(x_in, 'row', down)]
    ppermute x1, starting transfers between devices: 2.11 us -> 0.89 us  [shards(): high_mid = lax.ppermute(edge, 'row', up)]
  transfers between devices with their start and end apart: 13 -> 13, of which waited for: 11 -> 11; matrix products, arithmetic and copies ran while one was open for 1% -> 1% of each run, Pallas kernels for 4% -> 5%
where the time goes in v4:
time: 77.9 us; the launch traced here: 76.8 us
  starting transfers between devices  34.8 us (45%)
  waiting for transfers between devices  21.5 us (28%)
  Pallas kernels  18.6 us (24%)
  between operations  1 us (1%)
    pallas_call x1, Pallas kernels, shards(): call(functools.partial(block_kernel, count), 'block', (shape((streams, fr...  11.3 us
    all_to_all x1, starting transfers between devices, shards(): got = lax.all_to_all(send, 'dec', 0, 0, axis_index_groups=spread)  10.1 us
    all_to_all x1, starting transfers between devices, shards(): lax.all_to_all(back, ('section', 'dec'), 0, 0, axis_index_groups=gather)  7.42 us
    ppermute x2, waiting for transfers between devices, whole(): other = lax.ppermute(own, 'section', SWAP)  6.76 us
    ppermute x3, starting transfers between devices, shards(): lax.ppermute(stats, 'row', [(i, (i + shift) % bands) for i in range(bands)])  5.01 us
    all_to_all x1, waiting for transfers between devices, shards(): got = lax.all_to_all(send, 'dec', 0, 0, axis_index_groups=spread)  4 us
    ppermute x1, starting transfers between devices, shards(): low_mid = lax.ppermute(edges[:, :, rows - 1], 'row', down)  3.21 us
    ppermute x1, starting transfers between devices, shards(): high = lax.ppermute(x_in, 'row', up)  3.09 us
  transfers between devices with their start and end apart: 13, of which 11 were waited for; matrix products, arithmetic and copies ran while one was open for 1% of the time, Pallas kernels for 5%

profile of v4, /device:TPU:2, one launch (start us, length us, event | category | flops | bytes accessed | tf_op | source)
XLA Modules:
  0.0 76.8 jit_solution(4651100650049811995)
XLA Ops:
  0.6 0.0 copy-start.5
  0.6 0.0 copy-start.6
  0.7 0.0 copy-start.7
  0.7 0.0 copy-start.8
  0.7 0.0 copy-start.4
  0.7 2.0 %pack.1 = bf16[16,64,256]{2,1,0:T(8,128)(2,1)} custom-call(bf16[2,2,8,16,16]{4,3,2,1,0:T(8,128)(2,1)} %lat_ref.1, bf16[2,2,8,16,256]{4,3,2,1,0:T(8,128)(2,1)} %mid_ref.1), custom_call_target="tpu_custom_call" | custom-call | tf_op jit(solution)/shard_map/pack/pallas_call | solution.py:279
  2.7 10.1 %all-to-all-start = ((bf16[16,64,256]{2,1,0:T(8,128)(2,1)}), bf16[16,64,256]{2,1,0:T(8,128)(2,1)S(1)}, u32[]{:S(2)}, u32[]{:S(2)}) async-start(bf16[16,64,256]{2,1,0:T(8,128)(2,1)} %pack.1), calls=%async_computation | async-start | bytes 1048576 | tf_op jit(solution)/shard_map/all_to_all | solution.py:283
  12.9 0.0 copy-start
  12.9 0.0 copy-done.5
  12.9 1.5 %collective-permute-start.1 = (bf16[3,144,256]{2,1,0:T(8,128)(2,1)S(1)}, bf16[3,144,256]{2,1,0:T(8,128)(2,1)S(1)}, u32[]{:S(2)}, u32[]{:S(2)}) collective-permute-start(bf16[3,144,256]{2,1,0:T(8,128)(2,1)S(1)} %bitcast.30), channel_id=1, source_target_pairs={{0,128},{128,0},{1,129},{129,1},{2,130},{130,2},{3,131},{131,3},{4... | collective-permute-start | bytes 663560 | tf_op jit(solution)/shard_map/ppermute | solution.py:285
  14.4 0.0 copy-done.6
  14.4 0.0 copy-done.7
  14.4 0.0 copy-done.8
  14.4 0.7 collective-permute-start.2
  15.1 0.0 copy-done.4
  15.1 0.3 copy.25.weight_ref
  15.5 0.0 copy-done
  15.5 0.6 head.1.part_ref
  16.1 0.0 copy-start.9
  16.1 0.0 copy-start.1
  16.1 0.0 copy-start.3
  16.1 1.5 %collective-permute-start = (f32[8,16,128]{2,1,0:T(8,128)S(1)}, f32[8,16,128]{2,1,0:T(8,128)S(1)}, u32[]{:S(2)}, u32[]{:S(2)}) collective-permute-start(f32[8,16,128]{2,1,0:T(8,128)S(1)} %head.1.part_ref), channel_id=1, source_target_pairs={{0,128},{128,0},{1,129},{129,1},{2,130},{130,2},{3,131},{131,3},{4... | collective-permute-start | bytes 196616 | tf_op jit(solution)/shard_map/ppermute | solution.py:302
  17.6 6.8 %collective-permute-done.2 = f32[3,256]{1,0:T(4,128)S(1)} collective-permute-done((f32[3,256]{1,0:T(4,128)S(1)}, f32[3,256]{1,0:T(4,128)S(1)}, u32[]{:S(2)}, u32[]{:S(2)}) %collective-permute-start.2) | collective-permute-done | bytes 3104 | tf_op jit(solution)/shard_map/ppermute | solution.py:285
  24.4 0.0 collective-permute-done.1
  24.4 0.1 maximum_select_fusion
  24.5 0.1 pad.4.weight_ref
  24.6 1.5 %collective-permute-done.rest_ref = f32[8,16,128]{2,1,0:T(8,128)S(1)} collective-permute-done((f32[8,16,128]{2,1,0:T(8,128)S(1)}, f32[8,16,128]{2,1,0:T(8,128)S(1)}, u32[]{:S(2)}, u32[]{:S(2)}) %collective-permute-start) | collective-permute-done | bytes 65568 | tf_op jit(solution)/shard_map/ppermute | solution.py:302
  26.1 4.0 %all-to-all-done.got_ref = bf16[16,64,256]{2,1,0:T(8,128)(2,1)S(1)} async-done(((bf16[16,64,256]{2,1,0:T(8,128)(2,1)}), bf16[16,64,256]{2,1,0:T(8,128)(2,1)S(1)}, u32[]{:S(2)}, u32[]{:S(2)}) %all-to-all-start) | async-done | bytes 524320 | tf_op jit(solution)/shard_map/all_to_all | solution.py:283
  30.1 0.0 collective-permute-start.3
  30.1 0.0 copy-done.9
  30.1 0.1 reshape.39
  30.1 0.1 broadcast_in_dim.7
  30.2 0.1 reshape.40.bias_ref
  30.3 0.1 pad_add_fusion.me_ref
  30.4 1.6 %collective-permute-done.3.twin_ref = bf16[16,64,256]{2,1,0:T(8,128)(2,1)S(1)} collective-permute-done((bf16[16,64,256]{2,1,0:T(8,128)(2,1)S(1)}, bf16[16,64,256]{2,1,0:T(8,128)(2,1)S(1)}, u32[]{:S(2)}, u32[]{:S(2)}) %collective-permute-start.3) | collective-permute-done | bytes 524320 | tf_op jit(solution)/shard_map/ppermute | solution.py:305
  32.0 0.0 copy-done.1
  32.0 0.0 copy-done.3
  32.0 1.8 %pick.1 = (bf16[32,32,256]{2,1,0:T(8,128)(2,1)}, bf16[2,6,16,128]{3,2,1,0:T(8,128)(2,1)S(1)}) custom-call(s32[3]{0:T(128)S(1)} %pad_add_fusion.me_ref, s32[64]{0:T(128)S(1)} %copy-done.3, s32[2]{0:T(128)S(1)} %copy-done.1, bf16[16,64,256]{2,1,0:T(8,128)(2,1)S(1)} %all-to-all-done.got_ref, bf16[16,64,256]{2,1,0:T(8,128)(2,1)S(1)} %collective-permute-done.3.twin_ref, ...), custom_call_target="tpu_custom_call" | custom-call | tf_op jit(solution)/shard_map/pick/pallas_call | solution.py:306
  33.8 0.0 copy-start.2
  33.8 7.4 %all-to-all-start.1 = ((bf16[32,32,256]{2,1,0:T(8,128)(2,1)}), bf16[32,32,256]{2,1,0:T(8,128)(2,1)S(1)}, u32[]{:S(2)}, u32[]{:S(2)}) async-start(bf16[32,32,256]{2,1,0:T(8,128)(2,1)} %get-tuple-element.27), calls=%async_computation.1 | async-start | bytes 1048576 | tf_op jit(solution)/shard_map/all_to_all | solution.py:319
  41.2 3.1 %collective-permute-start.5 = (bf16[2,6,16,128]{3,2,1,0:T(8,128)(2,1)S(1)}, bf16[2,6,16,128]{3,2,1,0:T(8,128)(2,1)S(1)}, u32[]{:S(2)}, u32[]{:S(2)}) collective-permute-start(bf16[2,6,16,128]{3,2,1,0:T(8,128)(2,1)S(1)} %get-tuple-element.22.x_ref), channel_id=1, source_target_pairs={{1,0},{2,1},{3,2},{0,3},{5,4},{6,5},{7,6},{4,7},{9,8},{10,9},{11,1... | collective-permute-start | bytes 147464 | tf_op jit(solution)/shard_map/ppermute | solution.py:322
  44.3 1.3 %collective-permute-start.4 = (bf16[2,6,16,128]{3,2,1,0:T(8,128)(2,1)S(1)}, bf16[2,6,16,128]{3,2,1,0:T(8,128)(2,1)S(1)}, u32[]{:S(2)}, u32[]{:S(2)}) collective-permute-start(bf16[2,6,16,128]{3,2,1,0:T(8,128)(2,1)S(1)} %get-tuple-element.22.x_ref), channel_id=1, source_target_pairs={{0,1},{1,2},{2,3},{4,5},{5,6},{6,7},{8,9},{9,10},{10,11},{12,13},{... | collective-permute-start | bytes 147464 | tf_op jit(solution)/shard_map/ppermute | solution.py:321
  45.6 0.5 collective-permute-done.5.high_ref
  46.0 1.3 %collective-permute-done.4.low_ref = bf16[2,6,16,128]{3,2,1,0:T(8,128)(2,1)S(1)} collective-permute-done((bf16[2,6,16,128]{3,2,1,0:T(8,128)(2,1)S(1)}, bf16[2,6,16,128]{3,2,1,0:T(8,128)(2,1)S(1)}, u32[]{:S(2)}, u32[]{:S(2)}) %collective-permute-start.4) | collective-permute-done | bytes 49184 | tf_op jit(solution)/shard_map/ppermute | solution.py:321
  47.3 2.9 %first.1 = (bf16[2,4,10,16,512]{4,3,2,1,0:T(8,128)(2,1)S(1)}, f32[4,512]{1,0:T(4,128)S(1)}, bf16[2,2,8,16,16]{4,3,2,1,0:T(8,128)(2,1)}) custom-call(s32[3]{0:T(128)S(1)} %pad_add_fusion.me_ref, bf16[2,6,16,128]{3,2,1,0:T(8,128)(2,1)S(1)} %get-tuple-element.22.x_ref, bf16[2,6,16,128]{3,2,1,0:T(8,128)(2,1)S(1)} %collective-permute-done.4.low_ref, ...), custom_call_target="tpu_custom_call" | custom-call | tf_op jit(solution)/shard_map/first/pallas_call | solution.py:323
  50.2 3.7 %collective-permute-start.8 = (f32[4,512]{1,0:T(4,128)S(1)}, f32[4,512]{1,0:T(4,128)S(1)}, u32[]{:S(2)}, u32[]{:S(2)}) collective-permute-start(f32[4,512]{1,0:T(4,128)S(1)} %get-tuple-element.26.own_ref), channel_id=1, source_target_pairs={{0,3},{1,0},{2,1},{3,2},{4,7},{5,4},{6,5},{7,6},{8,11},{9,8},{10,9... | collective-permute-start | bytes 24584 | tf_op jit(solution)/shard_map/ppermute | solution.py:336
  53.9 0.7 collective-permute-start.7
  54.6 0.6 collective-permute-start.6
  55.2 2.0 %all-to-all-done.1.pieces_ref = bf16[32,32,256]{2,1,0:T(8,128)(2,1)S(1)} async-done(((bf16[32,32,256]{2,1,0:T(8,128)(2,1)}), bf16[32,32,256]{2,1,0:T(8,128)(2,1)S(1)}, u32[]{:S(2)}, u32[]{:S(2)}) %all-to-all-start.1) | async-done | bytes 524320 | tf_op jit(solution)/shard_map/all_to_all | solution.py:319
  57.3 0.0 collective-permute-done.8.back_ref
  57.3 1.8 %collective-permute-done.7.far_ref = f32[4,512]{1,0:T(4,128)S(1)} collective-permute-done((f32[4,512]{1,0:T(4,128)S(1)}, f32[4,512]{1,0:T(4,128)S(1)}, u32[]{:S(2)}, u32[]{:S(2)}) %collective-permute-start.7) | collective-permute-done | bytes 8224 | tf_op jit(solution)/shard_map/ppermute | solution.py:336
  59.1 0.4 collective-permute-done.6.near_ref
  59.5 0.9 %collective-permute-start.10 = (bf16[2,2,32,256]{3,2,1,0:T(8,128)(2,1)S(1)}, bf16[2,2,32,256]{3,2,1,0:T(8,128)(2,1)S(1)}, u32[]{:S(2)}, u32[]{:S(2)}) collective-permute-start(bf16[2,2,32,256]{3,2,1,0:T(8,128)(2,1)S(1)} %get-tuple-element.33), channel_id=1, source_target_pairs={{1,0},{2,1},{3,2},{0,3},{5,4},{6,5},{7,6},{4,7},{9,8},{10,9},{11,1... | collective-permute-start | bytes 196616 | tf_op jit(solution)/shard_map/ppermute | solution.py:343
  60.4 3.2 %collective-permute-start.9 = (bf16[2,2,32,256]{3,2,1,0:T(8,128)(2,1)S(1)}, bf16[2,2,32,256]{3,2,1,0:T(8,128)(2,1)S(1)}, u32[]{:S(2)}, u32[]{:S(2)}) collective-permute-start(bf16[2,2,32,256]{3,2,1,0:T(8,128)(2,1)S(1)} %get-tuple-element.37), channel_id=1, source_target_pairs={{0,1},{1,2},{2,3},{4,5},{5,6},{6,7},{8,9},{9,10},{10,11},{12,13},{... | collective-permute-start | bytes 196616 | tf_op jit(solution)/shard_map/ppermute | solution.py:341
  63.6 0.2 collective-permute-done.10.high_ref
  63.8 1.5 %collective-permute-done.9.low_ref = bf16[2,2,32,256]{3,2,1,0:T(8,128)(2,1)S(1)} collective-permute-done((bf16[2,2,32,256]{3,2,1,0:T(8,128)(2,1)S(1)}, bf16[2,2,32,256]{3,2,1,0:T(8,128)(2,1)S(1)}, u32[]{:S(2)}, u32[]{:S(2)}) %collective-permute-start.9) | collective-permute-done | bytes 65568 | tf_op jit(solution)/shard_map/ppermute | solution.py:341
  65.3 0.0 copy-done.2
  65.3 11.3 %block.1 = (bf16[2,4,8,16,256]{4,3,2,1,0:T(8,128)(2,1)}, bf16[2,2,8,16,256]{4,3,2,1,0:T(8,128)(2,1)}) custom-call(s32[3]{0:T(128)S(1)} %pad_add_fusion.me_ref, s32[2]{0:T(128)S(1)} %copy-done.1, bf16[2,4,10,16,512]{4,3,2,1,0:T(8,128)(2,1)S(1)} %get-tuple-element.25.first_ref, f32[4,512]{1,0:T(4,128)S(1)} %get-tuple-element.26.own_ref, ...), custom_call_target="tpu_custom_call" | custom-call | tf_op jit(solution)/shard_map/block/pallas_call | solution.py:346
  (8 shorter events, 0.1 us)
Async XLA Ops:
  0.6 12.2 %copy-start.5 = (bf16[3,3,3,16,256]{4,3,2,1,0:T(8,128)(2,1)S(1)}, bf16[3,3,3,16,256]{4,3,2,1,0:T(8,128)(2,1)}, u32[]{:S(2)}) copy-start(bf16[3,3,3,16,256]{4,3,2,1,0:T(8,128)(2,1)} %param.20) | copy-start | bytes 663556
  0.6 13.8 %copy-start.6 = (f32[256]{0:T(256)S(1)}, f32[256]{0:T(256)}, u32[]{:S(2)}) copy-start(f32[256]{0:T(256)} %param.23) | copy-start | bytes 3076
  0.7 13.8 %copy-start.7 = (f32[256]{0:T(256)S(1)}, f32[256]{0:T(256)}, u32[]{:S(2)}) copy-start(f32[256]{0:T(256)} %param.22) | copy-start | bytes 3076
  0.7 13.8 %copy-start.8 = (f32[256]{0:T(256)S(1)}, f32[256]{0:T(256)}, u32[]{:S(2)}) copy-start(f32[256]{0:T(256)} %param.21) | copy-start | bytes 3076
  0.7 14.4 %copy-start.4 = (bf16[2560,64]{0,1:T(8,128)(2,1)S(1)}, bf16[2560,64]{0,1:T(8,128)(2,1)}, u32[]{:S(2)}) copy-start(bf16[2560,64]{0,1:T(8,128)(2,1)} %param.14) | copy-start | bytes 983044
  2.7 27.3 %all-to-all-start = ((bf16[16,64,256]{2,1,0:T(8,128)(2,1)}), bf16[16,64,256]{2,1,0:T(8,128)(2,1)S(1)}, u32[]{:S(2)}, u32[]{:S(2)}) async-start(bf16[16,64,256]{2,1,0:T(8,128)(2,1)} %pack.1), calls=%async_computation | async-start | bytes 1048576 | tf_op jit(solution)/shard_map/all_to_all | solution.py:283
  12.9 2.6 %copy-start = (bf16[2,4,4,8,2560]{4,3,2,1,0:T(8,128)(2,1)S(1)}, bf16[2,4,4,8,2560]{4,3,2,1,0:T(8,128)(2,1)}, u32[]{:S(2)}) copy-start(bf16[2,4,4,8,2560]{4,3,2,1,0:T(8,128)(2,1)} %param.13) | copy-start | bytes 3932164
  12.9 11.5 %collective-permute-start.1 = (bf16[3,144,256]{2,1,0:T(8,128)(2,1)S(1)}, bf16[3,144,256]{2,1,0:T(8,128)(2,1)S(1)}, u32[]{:S(2)}, u32[]{:S(2)}) collective-permute-start(bf16[3,144,256]{2,1,0:T(8,128)(2,1)S(1)} %bitcast.30), channel_id=1, source_target_pairs={{0,128},{128,0},{1,129},{129,1},{2,130},{130,2},{3,131},{131,3},{4... | collective-permute-start | bytes 663560 | tf_op jit(solution)/shard_map/ppermute | solution.py:285
  14.4 9.9 %collective-permute-start.2 = (f32[3,256]{1,0:T(4,128)S(1)}, f32[3,256]{1,0:T(4,128)S(1)}, u32[]{:S(2)}, u32[]{:S(2)}) collective-permute-start(f32[3,256]{1,0:T(4,128)S(1)} %pad_maximum_fusion), channel_id=1, source_target_pairs={{0,128},{128,0},{1,129},{129,1},{2,130},{130,2},{3,131},{131,3},{4... | collective-permute-start | bytes 9224 | tf_op jit(solution)/shard_map/ppermute | solution.py:285
  16.1 14.0 %copy-start.9 = (f32[64]{0:T(128)S(1)}, f32[64]{0:T(128)}, u32[]{:S(2)}) copy-start(f32[64]{0:T(128)} %param.15) | copy-start | bytes 772
  16.1 15.9 %copy-start.1 = (s32[2]{0:T(128)S(1)}, s32[2]{0:T(128)}, u32[]{:S(2)}) copy-start(s32[2]{0:T(128)} %span_ref.3) | copy-start | bytes 28
  16.1 15.9 %copy-start.3 = (s32[64]{0:T(128)S(1)}, s32[64]{0:T(128)}, u32[]{:S(2)}) copy-start(s32[64]{0:T(128)} %moves_ref.1) | copy-start | bytes 772
  16.1 10.0 %collective-permute-start = (f32[8,16,128]{2,1,0:T(8,128)S(1)}, f32[8,16,128]{2,1,0:T(8,128)S(1)}, u32[]{:S(2)}, u32[]{:S(2)}) collective-permute-start(f32[8,16,128]{2,1,0:T(8,128)S(1)} %head.1.part_ref), channel_id=1, source_target_pairs={{0,128},{128,0},{1,129},{129,1},{2,130},{130,2},{3,131},{131,3},{4... | collective-permute-start | bytes 196616 | tf_op jit(solution)/shard_map/ppermute | solution.py:302
  30.1 1.9 %collective-permute-start.3 = (bf16[16,64,256]{2,1,0:T(8,128)(2,1)S(1)}, bf16[16,64,256]{2,1,0:T(8,128)(2,1)S(1)}, u32[]{:S(2)}, u32[]{:S(2)}) collective-permute-start(bf16[16,64,256]{2,1,0:T(8,128)(2,1)S(1)} %all-to-all-done.got_ref), channel_id=1, source_target_pairs={{0,4},{4,0},{8,12},{12,8},{16,20},{20,16},{24,28},{28,24},{32,36},... | collective-permute-start | bytes 1572872 | tf_op jit(solution)/shard_map/ppermute | solution.py:305
  33.8 31.5 %copy-start.2 = (f32[256]{0:T(256)S(1)}, f32[256]{0:T(256)}, u32[]{:S(2)}) copy-start(f32[256]{0:T(256)} %param.25) | copy-start | bytes 3076
  33.8 23.5 %all-to-all-start.1 = ((bf16[32,32,256]{2,1,0:T(8,128)(2,1)}), bf16[32,32,256]{2,1,0:T(8,128)(2,1)S(1)}, u32[]{:S(2)}, u32[]{:S(2)}) async-start(bf16[32,32,256]{2,1,0:T(8,128)(2,1)} %get-tuple-element.27), calls=%async_computation.1 | async-start | bytes 1048576 | tf_op jit(solution)/shard_map/all_to_all | solution.py:319
  41.2 4.8 %collective-permute-start.5 = (bf16[2,6,16,128]{3,2,1,0:T(8,128)(2,1)S(1)}, bf16[2,6,16,128]{3,2,1,0:T(8,128)(2,1)S(1)}, u32[]{:S(2)}, u32[]{:S(2)}) collective-permute-start(bf16[2,6,16,128]{3,2,1,0:T(8,128)(2,1)S(1)} %get-tuple-element.22.x_ref), channel_id=1, source_target_pairs={{1,0},{2,1},{3,2},{0,3},{5,4},{6,5},{7,6},{4,7},{9,8},{10,9},{11,1... | collective-permute-start | bytes 147464 | tf_op jit(solution)/shard_map/ppermute | solution.py:322
  44.3 3.0 %collective-permute-start.4 = (bf16[2,6,16,128]{3,2,1,0:T(8,128)(2,1)S(1)}, bf16[2,6,16,128]{3,2,1,0:T(8,128)(2,1)S(1)}, u32[]{:S(2)}, u32[]{:S(2)}) collective-permute-start(bf16[2,6,16,128]{3,2,1,0:T(8,128)(2,1)S(1)} %get-tuple-element.22.x_ref), channel_id=1, source_target_pairs={{0,1},{1,2},{2,3},{4,5},{5,6},{6,7},{8,9},{9,10},{10,11},{12,13},{... | collective-permute-start | bytes 147464 | tf_op jit(solution)/shard_map/ppermute | solution.py:321
  50.2 7.0 %collective-permute-start.8 = (f32[4,512]{1,0:T(4,128)S(1)}, f32[4,512]{1,0:T(4,128)S(1)}, u32[]{:S(2)}, u32[]{:S(2)}) collective-permute-start(f32[4,512]{1,0:T(4,128)S(1)} %get-tuple-element.26.own_ref), channel_id=1, source_target_pairs={{0,3},{1,0},{2,1},{3,2},{4,7},{5,4},{6,5},{7,6},{8,11},{9,8},{10,9... | collective-permute-start | bytes 24584 | tf_op jit(solution)/shard_map/ppermute | solution.py:336
  53.9 5.2 %collective-permute-start.7 = (f32[4,512]{1,0:T(4,128)S(1)}, f32[4,512]{1,0:T(4,128)S(1)}, u32[]{:S(2)}, u32[]{:S(2)}) collective-permute-start(f32[4,512]{1,0:T(4,128)S(1)} %get-tuple-element.26.own_ref), channel_id=1, source_target_pairs={{0,2},{1,3},{2,0},{3,1},{4,6},{5,7},{6,4},{7,5},{8,10},{9,11},{10,... | collective-permute-start | bytes 24584 | tf_op jit(solution)/shard_map/ppermute | solution.py:336
  54.6 4.9 %collective-permute-start.6 = (f32[4,512]{1,0:T(4,128)S(1)}, f32[4,512]{1,0:T(4,128)S(1)}, u32[]{:S(2)}, u32[]{:S(2)}) collective-permute-start(f32[4,512]{1,0:T(4,128)S(1)} %get-tuple-element.26.own_ref), channel_id=1, source_target_pairs={{0,1},{1,2},{2,3},{3,0},{4,5},{5,6},{6,7},{7,4},{8,9},{9,10},{10,1... | collective-permute-start | bytes 24584 | tf_op jit(solution)/shard_map/ppermute | solution.py:336
  59.5 4.3 %collective-permute-start.10 = (bf16[2,2,32,256]{3,2,1,0:T(8,128)(2,1)S(1)}, bf16[2,2,32,256]{3,2,1,0:T(8,128)(2,1)S(1)}, u32[]{:S(2)}, u32[]{:S(2)}) collective-permute-start(bf16[2,2,32,256]{3,2,1,0:T(8,128)(2,1)S(1)} %get-tuple-element.33), channel_id=1, source_target_pairs={{1,0},{2,1},{3,2},{0,3},{5,4},{6,5},{7,6},{4,7},{9,8},{10,9},{11,1... | collective-permute-start | bytes 196616 | tf_op jit(solution)/shard_map/ppermute | solution.py:343
  60.4 4.9 %collective-permute-start.9 = (bf16[2,2,32,256]{3,2,1,0:T(8,128)(2,1)S(1)}, bf16[2,2,32,256]{3,2,1,0:T(8,128)(2,1)S(1)}, u32[]{:S(2)}, u32[]{:S(2)}) collective-permute-start(bf16[2,2,32,256]{3,2,1,0:T(8,128)(2,1)S(1)} %get-tuple-element.37), channel_id=1, source_target_pairs={{0,1},{1,2},{2,3},{4,5},{5,6},{6,7},{8,9},{9,10},{10,11},{12,13},{... | collective-permute-start | bytes 196616 | tf_op jit(solution)/shard_map/ppermute | solution.py:341
